TPU v7x, 128 devices: a whole 4x4x4 slice. The times are simulated.
128 devices in a mesh: pipe: 8 (over x_hi, y), expert: 16 (over z, x_lo, core).
Axes of the slice: x: 4 (x_hi: 2, x_lo: 2; x = x_hi * 2 + x_lo), y: 4, z: 4, core: 2. Of those that a mesh axis runs over, the one named last changes fastest.
Arguments:
- x_fwd: bfloat16 [16384, 1536], P(('pipe', 'expert')), may hold values from -6 to 6
- gate_fwd: float32 [16384, 6], P(('pipe', 'expert')), may hold values from 0.05 to 0.4
- route_fwd: int32 [16384, 6], P(('pipe', 'expert')), may hold values from 0 to 31, all different within a row; in each aligned block of 128 rows (0 to 127, 128 to 255, ...) at most 32 rows name the same one
- x_bwd: bfloat16 [16384, 1536], P(('pipe', 'expert')), may hold values from -6 to 6
- gate_bwd: float32 [16384, 6], P(('pipe', 'expert')), may hold values from 0.05 to 0.4
- route_bwd: int32 [16384, 6], P(('pipe', 'expert')), may hold values from 0 to 31, all different within a row; in each aligned block of 128 rows (0 to 127, 128 to 255, ...) at most 32 rows name the same one
- cotangent: bfloat16 [16384, 1536], P(('pipe', 'expert')), may hold values from -6 to 6
- norm_gain: float32 [1536], replicated, may hold values from 0.5 to 1.5
- w_gate_up: bfloat16 [8, 32, 1536, 1536], P('pipe', 'expert'), as said below
- w_down: bfloat16 [8, 32, 768, 1536], P('pipe', 'expert'), as said below
Outputs:
- y_fwd: bfloat16 [16384, 1536], P(('pipe', 'expert'))
- dx_bwd: bfloat16 [16384, 1536], P(('pipe', 'expert'))
- grad_gate_up: bfloat16 [8, 16, 1536, 1536], P('pipe', 'expert')
- grad_down: bfloat16 [8, 16, 768, 1536], P('pipe', 'expert')
Inputs may be any that keep to these rules, and one draw needn't show every extreme that they name: `route_fwd`: each row names 6 different experts; in the 128 rows of one group no expert is named more than 32 times. `route_bwd`: each row names 6 different experts; in the 128 rows of one group no expert is named more than 32 times. w_gate_up[p] equals w_gate_up[7 - p]. w_down[p] equals w_down[7 - p].
All inputs are finite; a program needn't handle non-finite values.
Results may differ from a plain program's by a relative error of at most 0.0078.
Values may be sent and summed in bfloat16 or wider, within the bound.
A program may use at most 192 MiB of HBM per device.

v0:
```python
import jax
import jax.numpy as jnp
from jax import lax
from jax.sharding import PartitionSpec as P

norm_eps = 1e-06


def from_partner(value, axis, bit):
    return lax.ppermute(value, axis, [(i, i ^ 1 << bit) for i in range(lax.axis_size(axis))])


def normalize(inputs):
    values = inputs.astype(jnp.float32)
    scale = lax.rsqrt(jnp.mean(values * values, axis=-1, keepdims=True) + norm_eps)
    return (values * scale, scale)


def destinations(routes, expert_count, capacity):
    flat_routes = routes.reshape(-1)
    onehot = (flat_routes[:, None] == jnp.arange(expert_count, dtype=jnp.int32)[None, :]).astype(
        jnp.int32
    )
    before = jnp.cumsum(onehot, axis=0) - onehot
    slot = jnp.sum(before * onehot, axis=1)
    return (flat_routes * capacity + slot).reshape(routes.shape)


def place_rows(values, dest, slot_total):
    flat_values = values.reshape(-1, values.shape[-1])
    return (
        jnp.zeros((slot_total, values.shape[-1]), values.dtype)
        .at[dest.reshape(-1)]
        .set(flat_values)
    )


def expert_forward(inputs, weight_gu, weight_dn):
    hidden_units = weight_dn.shape[1]
    both_parts = jnp.einsum("secd,edf->secf", inputs, weight_gu, preferred_element_type=jnp.float32)
    gate_pre = both_parts[..., :hidden_units]
    up_pre = both_parts[..., hidden_units:]
    hidden = (jax.nn.silu(gate_pre) * up_pre).astype(jnp.bfloat16)
    return jnp.einsum(
        "secf,efd->secd", hidden, weight_dn, preferred_element_type=jnp.float32
    ).astype(jnp.bfloat16)


def expert_backward(inputs, cot_rows, weight_gu, weight_dn):
    hidden_units = weight_dn.shape[1]
    both_parts = jnp.einsum("secd,edf->secf", inputs, weight_gu, preferred_element_type=jnp.float32)
    gate_pre = both_parts[..., :hidden_units]
    up_pre = both_parts[..., hidden_units:]
    squash = jax.nn.sigmoid(gate_pre)
    activated = gate_pre * squash
    hidden = (activated * up_pre).astype(jnp.bfloat16)
    back_hidden = jnp.einsum(
        "secd,efd->secf", cot_rows, weight_dn, preferred_element_type=jnp.float32
    )
    d_gate = back_hidden * up_pre * squash * (1.0 + gate_pre * (1.0 - squash))
    d_up = back_hidden * activated
    d_both = jnp.concatenate([d_gate, d_up], axis=-1).astype(jnp.bfloat16)
    d_inputs = jnp.einsum(
        "secf,edf->secd", d_both, weight_gu, preferred_element_type=jnp.float32
    ).astype(jnp.bfloat16)
    grad_dn = jnp.einsum(
        "secf,secd->efd", hidden, cot_rows, preferred_element_type=jnp.float32
    ).astype(jnp.bfloat16)
    grad_gu = jnp.einsum(
        "secd,secf->edf", inputs, d_both, preferred_element_type=jnp.float32
    ).astype(jnp.bfloat16)
    return (d_inputs, grad_gu, grad_dn)


def per_device(
    x_fwd, gate_fwd, route_fwd, x_bwd, gate_bwd, route_bwd, cotangent, norm_gain, w_gate_up, w_down
):
    group_count = lax.axis_size("expert")
    local_count = w_gate_up.shape[1]
    expert_count = local_count * group_count
    token_count = x_fwd.shape[0]
    model_width = x_fwd.shape[1]
    pick_count = route_fwd.shape[1]
    capacity = token_count * pick_count * 4 // (3 * expert_count)
    slot_total = expert_count * capacity
    buffer_shape = (group_count, local_count, capacity, model_width)
    row_shape = (token_count, pick_count, model_width)
    weight_gu = w_gate_up[0]
    weight_dn = w_down[0]
    fwd_normed = (normalize(x_fwd)[0] * norm_gain).astype(jnp.bfloat16)
    dest_fwd = destinations(route_fwd, expert_count, capacity)
    send_fwd = place_rows(
        jnp.broadcast_to(fwd_normed[:, None, :], row_shape), dest_fwd, slot_total
    ).reshape(buffer_shape)
    bwd_hat, bwd_scale = normalize(x_bwd)
    bwd_normed = (bwd_hat * norm_gain).astype(jnp.bfloat16)
    scaled_cot = (gate_bwd[:, :, None] * cotangent.astype(jnp.float32)[:, None, :]).astype(
        jnp.bfloat16
    )
    dest_bwd = destinations(route_bwd, expert_count, capacity)
    send_inputs = place_rows(
        jnp.broadcast_to(bwd_normed[:, None, :], row_shape), dest_bwd, slot_total
    ).reshape(buffer_shape)
    send_cot = place_rows(scaled_cot, dest_bwd, slot_total).reshape(buffer_shape)
    recv_fwd = lax.all_to_all(send_fwd, "expert", split_axis=0, concat_axis=0, tiled=True)
    recv_inputs, recv_cot = (
        lax.all_to_all(send_inputs, "expert", split_axis=0, concat_axis=0, tiled=True),
        lax.all_to_all(send_cot, "expert", split_axis=0, concat_axis=0, tiled=True),
    )
    out_fwd = expert_forward(recv_fwd, weight_gu, weight_dn)
    back_fwd = lax.all_to_all(out_fwd, "expert", split_axis=0, concat_axis=0, tiled=True)
    d_inputs, grad_gu, grad_dn = expert_backward(recv_inputs, recv_cot, weight_gu, weight_dn)
    back_dh = lax.all_to_all(d_inputs, "expert", split_axis=0, concat_axis=0, tiled=True)
    picked = back_fwd.reshape(slot_total, model_width)[dest_fwd]
    y_fwd = jnp.sum(picked.astype(jnp.float32) * gate_fwd[:, :, None], axis=1).astype(jnp.bfloat16)
    dh_sum = jnp.sum(back_dh.reshape(slot_total, model_width)[dest_bwd].astype(jnp.float32), axis=1)
    scaled_dh = norm_gain * dh_sum
    dx_bwd = (
        bwd_scale * (scaled_dh - bwd_hat * jnp.mean(bwd_hat * scaled_dh, axis=-1, keepdims=True))
    ).astype(jnp.bfloat16)
    section_index = lax.axis_index("pipe")
    section_count = lax.axis_size("pipe")
    upper_half = (section_index >= section_count // 2).astype(jnp.int32)
    half_local = local_count // 2
    keep_gu = lax.dynamic_slice_in_dim(grad_gu, upper_half * half_local, half_local, 0)
    give_gu = lax.dynamic_slice_in_dim(grad_gu, (1 - upper_half) * half_local, half_local, 0)
    keep_dn = lax.dynamic_slice_in_dim(grad_dn, upper_half * half_local, half_local, 0)
    give_dn = lax.dynamic_slice_in_dim(grad_dn, (1 - upper_half) * half_local, half_local, 0)
    bit_count = section_count.bit_length() - 1
    for bit_number in range(bit_count):
        give_gu = from_partner(give_gu, "pipe", bit_number)
    down_bits = list(range(bit_count))
    for bit_number in down_bits:
        give_dn = from_partner(give_dn, "pipe", bit_number)
    out_gu = (keep_gu.astype(jnp.float32) + give_gu.astype(jnp.float32)).astype(jnp.bfloat16)
    out_dn = (keep_dn.astype(jnp.float32) + give_dn.astype(jnp.float32)).astype(jnp.bfloat16)
    return (y_fwd, dx_bwd, out_gu[None], out_dn[None])


def solution(mesh):
    return jax.shard_map(
        per_device,
        mesh=mesh,
        in_specs=(
            P(("pipe", "expert"), None),
            P(("pipe", "expert"), None),
            P(("pipe", "expert"), None),
            P(("pipe", "expert"), None),
            P(("pipe", "expert"), None),
            P(("pipe", "expert"), None),
            P(("pipe", "expert"), None),
            P(),
            P("pipe", "expert", None, None),
            P("pipe", "expert", None, None),
        ),
        out_specs=(
            P(("pipe", "expert"), None),
            P(("pipe", "expert"), None),
            P("pipe", "expert", None, None),
            P("pipe", "expert", None, None),
        ),
        check_vma=False,
    )
```

profile of v0, /device:TPU:1, one launch (start us, length us, event | category | flops | bytes accessed | tf_op | source)
XLA Modules:
  0.0 646.9 jit_solution(5019076254783176583)
XLA Ops:
  0.6 0.8 copy.37
  1.7 1.2 fusion.53
  2.9 1.2 fusion.61
  4.0 1.7 reduce-window.16
  5.8 0.3 slice_reduce_fusion
  6.3 0.6 compare_select_fusion
  7.0 0.1 mul.162
  7.1 1.2 fusion.56
  8.3 0.4 broadcast_in_dim.14
  8.7 2.2 reshape.200
  10.9 8.9 %scatter_custom_fusion.2 = bf16[1024,1536]{1,0:T(8,128)(2,1)} fusion(s32[768]{0:T(1024)S(1)} %fusion.72, bf16[768,1536]{1,0:T(8,128)(2,1)} %reshape.200, bf16[]{:T(256)} %constant.14.clone.1), kind=kCustom, calls=%fused_computation.49 | custom fusion | bytes 3146240 | tf_op jit(solution)/shard_map/scatter | solution.py:34
  19.8 8.3 %all-to-all-start.3 = ((bf16[16,2,32,1536]{3,2,1,0:T(8,128)(2,1)}), bf16[16,2,32,1536]{3,2,1,0:T(8,128)(2,1)S(1)}, u32[]{:S(2)}, u32[]{:S(2)}) async-start(bf16[16,2,32,1536]{3,2,1,0:T(8,128)(2,1)} %bitcast.15), calls=%async_computation.3 | async-start | bytes 6291456 | tf_op jit(solution)/shard_map/all_to_all | solution.py:107
  28.1 0.7 copy.41
  28.8 1.0 mul.164
  29.8 3.5 mul.166
  33.3 6.5 %mul.167 = f32[768,1536]{1,0:T(8,128)} reshape(f32[128,6,1536]{2,1,0:T(8,128)} %mul.166) | data formatting | bytes 9437184 | tf_op jit(solution)/shard_map/mul | solution.py:97
  39.8 13.3 %scatter_custom_fusion.1 = bf16[1024,1536]{1,0:T(8,128)(2,1)} fusion(s32[768]{0:T(1024)S(1)} %fusion.72, f32[768,1536]{1,0:T(8,128)} %mul.167, f32[768]{0:T(1024)S(1)} %mul.164, bf16[]{:T(256)} %constant.14.clone.1), kind=kCustom, calls=%fused_computation.45 | custom fusion | flops 2359296 | bytes 7868418 | tf_op jit(solution)/shard_map/scatter | solution.py:34
  53.0 13.3 %all-to-all-done.3 = bf16[16,2,32,1536]{3,2,1,0:T(8,128)(2,1)S(1)} async-done(((bf16[16,2,32,1536]{3,2,1,0:T(8,128)(2,1)}), bf16[16,2,32,1536]{3,2,1,0:T(8,128)(2,1)S(1)}, u32[]{:S(2)}, u32[]{:S(2)}) %all-to-all-start.3) | async-done | bytes 3145760 | tf_op jit(solution)/shard_map/all_to_all | solution.py:107
  66.3 1.7 copy-done.4
  68.0 5.0 all-to-all-start.2
  73.0 11.1 %fusion.14 = f32[16,2,32,1536]{3,2,0,1:T(8,128)} fusion(bf16[1,2,1536,1536]{3,2,1,0:T(8,128)(2,1)} %param.18, bf16[16,2,32,1536]{3,2,1,0:T(8,128)(2,1)} %copy-done.4), kind=kOutput, calls=%fused_computation.23 | convolution fusion | flops 4831838208 | bytes 18874368 | tf_op jit(solution)/shard_map/secd,edf->secf/dot_general | solution.py:51
  84.1 27.2 %all-to-all-done.2 = bf16[16,2,32,1536]{3,2,1,0:T(8,128)(2,1)S(1)} async-done(((bf16[16,2,32,1536]{3,2,1,0:T(8,128)(2,1)}), bf16[16,2,32,1536]{3,2,1,0:T(8,128)(2,1)S(1)}, u32[]{:S(2)}, u32[]{:S(2)}) %all-to-all-start.2) | async-done | bytes 3145760 | tf_op jit(solution)/shard_map/all_to_all | solution.py:108
  111.3 7.9 %fusion.32 = (bf16[16,2,32,768]{3,2,0,1:T(8,128)(2,1)S(1)}, bf16[16,2,32,768]{3,2,0,1:T(8,128)(2,1)S(1)}) fusion(f32[16,2,32,1536]{3,2,0,1:T(8,128)} %fusion.14, bf16[1,2,768,1536]{3,2,1,0:T(8,128)(2,1)} %param.19, bf16[16,2,32,1536]{3,2,1,0:T(8,128)(2,1)S(1)} %all-to-all-done.2), kind=kOutput, calls=%fused_computation.35 | convolution fusion | flops 2426142720 | bytes 17301504 | tf_op jit(solution)/shard_map/secd,efd->secf/dot_general | solution.py:57
  119.3 5.4 bitcast_convert_fusion
  124.7 2.7 constant_dynamic-slice_fusion.1
  127.4 2.3 copy-done
  129.7 1.3 collective-permute-start
  131.5 8.7 %fusion.23 = bf16[16,2,32,1536]{3,2,0,1:T(8,128)(2,1)S(1)} fusion(bf16[1,2,1536,1536]{3,2,1,0:T(8,128)(2,1)} %param.18, bf16[16,2,32,768]{3,2,0,1:T(8,128)(2,1)} %copy-done.14, bf16[16,2,32,768]{3,2,0,1:T(8,128)(2,1)} %copy-done.13), kind=kOutput, calls=%fused_computation.26 | convolution fusion | flops 4839702528 | bytes 15728640 | tf_op jit(solution)/shard_map/secf,edf->secd/dot_general | solution.py:63
  140.2 2.0 copy.44
  142.2 4.7 all-to-all-start.4
  146.9 6.5 %bitcast_convert_fusion.1 = bf16[2,768,1536]{2,1,0:T(8,128)(2,1)S(1)} fusion(bf16[16,2,32,1536]{3,2,1,0:T(8,128)(2,1)} %copy-done.3, f32[16,2,32,1536]{3,2,0,1:T(8,128)} %fusion.14), kind=kOutput, calls=%fused_computation.6 | convolution fusion | flops 2422996992 | bytes 14155776 | tf_op jit(solution)/shard_map/secf,secd->efd/dot_general | solution.py:66
  153.4 2.1 copy-done.2
  155.5 1.6 constant_dynamic-slice_fusion
  157.1 0.2 collective-permute-start.3
  157.3 75.2 %collective-permute-done = bf16[1,1536,1536]{2,1,0:T(8,128)(2,1)} collective-permute-done((bf16[1,1536,1536]{2,1,0:T(8,128)(2,1)}, bf16[1,1536,1536]{2,1,0:T(8,128)(2,1)}, u32[]{:S(2)}, u32[]{:S(2)}) %collective-permute-start) | collective-permute-done | bytes 4718624 | tf_op jit(solution)/shard_map/ppermute | solution.py:10
  232.5 3.1 collective-permute-start.1
  235.6 1.7 reduce-window.14
  237.3 0.3 slice_reduce_fusion.1
  237.9 0.1 mul.148
  238.1 3.8 gather_fusion.1
  241.9 4.9 reshape.209
  246.8 4.7 reduce_sum.80
  251.6 0.3 fusion.57
  251.8 1.0 fusion.60
  252.8 0.4 broadcast_in_dim.12
  253.2 2.2 reshape.184
  255.4 8.8 %scatter_custom_fusion = bf16[1024,1536]{1,0:T(8,128)(2,1)} fusion(s32[768]{0:T(1024)S(1)} %fusion.71, bf16[768,1536]{1,0:T(8,128)(2,1)} %reshape.184, bf16[]{:T(256)} %constant.14.clone.1), kind=kCustom, calls=%fused_computation.52 | custom fusion | bytes 3146240 | tf_op jit(solution)/shard_map/scatter | solution.py:34
  264.3 7.0 %all-to-all-start = ((bf16[16,2,32,1536]{3,2,1,0:T(8,128)(2,1)}), bf16[16,2,32,1536]{3,2,1,0:T(8,128)(2,1)S(1)}, u32[]{:S(2)}, u32[]{:S(2)}) async-start(bf16[16,2,32,1536]{3,2,1,0:T(8,128)(2,1)} %bitcast.1), calls=%async_computation | async-start | bytes 6291456 | tf_op jit(solution)/shard_map/all_to_all | solution.py:105
  271.2 11.8 %collective-permute-done.3 = bf16[1,768,1536]{2,1,0:T(8,128)(2,1)} collective-permute-done((bf16[1,768,1536]{2,1,0:T(8,128)(2,1)}, bf16[1,768,1536]{2,1,0:T(8,128)(2,1)}, u32[]{:S(2)}, u32[]{:S(2)}) %collective-permute-start.3) | collective-permute-done | bytes 2359328 | tf_op jit(solution)/shard_map/ppermute | solution.py:10
  283.0 2.9 collective-permute-start.4
  285.9 151.2 %collective-permute-done.4 = bf16[1,768,1536]{2,1,0:T(8,128)(2,1)} collective-permute-done((bf16[1,768,1536]{2,1,0:T(8,128)(2,1)}, bf16[1,768,1536]{2,1,0:T(8,128)(2,1)}, u32[]{:S(2)}, u32[]{:S(2)}) %collective-permute-start.4) | collective-permute-done | bytes 2359328 | tf_op jit(solution)/shard_map/ppermute | solution.py:10
  437.2 2.5 collective-permute-start.5
  439.6 0.7 collective-permute-start.2
  440.3 7.6 %fusion.11 = f32[16,2,32,1536]{3,2,0,1:T(8,128)S(1)} fusion(bf16[1,2,1536,1536]{3,2,1,0:T(8,128)(2,1)} %param.18, bf16[16,2,32,1536]{3,2,1,0:T(8,128)(2,1)S(1)} %all-to-all-done), kind=kOutput, calls=%fused_computation.22 | convolution fusion | flops 4831838208 | bytes 18874368 | tf_op jit(solution)/shard_map/secd,edf->secf/dot_general | solution.py:40
  447.9 5.2 fusion.26
  453.1 2.0 copy.35
  455.1 6.0 all-to-all-start.1
  461.4 28.6 %collective-permute-done.5 = bf16[1,768,1536]{2,1,0:T(8,128)(2,1)} collective-permute-done((bf16[1,768,1536]{2,1,0:T(8,128)(2,1)}, bf16[1,768,1536]{2,1,0:T(8,128)(2,1)}, u32[]{:S(2)}, u32[]{:S(2)}) %collective-permute-start.5) | collective-permute-done | bytes 2359328 | tf_op jit(solution)/shard_map/ppermute | solution.py:10
  489.9 4.4 fusion.41
  494.3 130.4 %all-to-all-done.1 = bf16[16,2,32,1536]{3,2,1,0:T(8,128)(2,1)S(1)} async-done(((bf16[16,2,32,1536]{3,2,1,0:T(8,128)(2,1)}), bf16[16,2,32,1536]{3,2,1,0:T(8,128)(2,1)S(1)}, u32[]{:S(2)}, u32[]{:S(2)}) %all-to-all-start.1) | async-done | bytes 3145760 | tf_op jit(solution)/shard_map/all_to_all | solution.py:111
  624.8 3.8 gather_fusion
  628.6 4.9 reshape.208
  633.5 5.9 multiply_reduce_fusion
  639.4 7.3 %fusion.6 = bf16[1,1,1536,1536]{3,2,1,0:T(8,128)(2,1)} fusion(bf16[1,1536,1536]{2,1,0:T(8,128)(2,1)} %collective-permute-done.2, bf16[2,1536,1536]{2,1,0:T(8,128)(2,1)} %copy-done, s32[]{:T(128)S(6)} %select_n.39), kind=kLoop, calls=%fused_computation.15 | loop fusion | flops 9437184 | bytes 14155780 | tf_op jit(solution)/shard_map/broadcast_in_dim | solution.py:137
  (54 shorter events, 1.7 us)
Async XLA Ops:
  19.8 8.3 %copy-start.10 = (f32[128,6]{0,1:T(8,128)S(1)}, f32[128,6]{0,1:T(8,128)}, u32[]{:S(2)}) copy-start(f32[128,6]{0,1:T(8,128)} %param.14) | copy-start | bytes 9220
  19.8 10.0 %copy-start.7 = (bf16[128,1536]{1,0:T(8,128)(2,1)S(1)}, bf16[128,1536]{1,0:T(8,128)(2,1)}, u32[]{:S(2)}) copy-start(bf16[128,1536]{1,0:T(8,128)(2,1)} %param.16) | copy-start | bytes 1179652
  19.8 46.5 %all-to-all-start.3 = ((bf16[16,2,32,1536]{3,2,1,0:T(8,128)(2,1)}), bf16[16,2,32,1536]{3,2,1,0:T(8,128)(2,1)S(1)}, u32[]{:S(2)}, u32[]{:S(2)}) async-start(bf16[16,2,32,1536]{3,2,1,0:T(8,128)(2,1)} %bitcast.15), calls=%async_computation.3 | async-start | bytes 6291456 | tf_op jit(solution)/shard_map/all_to_all | solution.py:107
  66.3 1.7 copy-start.4
  68.0 43.3 %all-to-all-start.2 = ((bf16[16,2,32,1536]{3,2,1,0:T(8,128)(2,1)}), bf16[16,2,32,1536]{3,2,1,0:T(8,128)(2,1)S(1)}, u32[]{:S(2)}, u32[]{:S(2)}) async-start(bf16[16,2,32,1536]{3,2,1,0:T(8,128)(2,1)} %bitcast.12), calls=%async_computation.2 | async-start | bytes 6291456 | tf_op jit(solution)/shard_map/all_to_all | solution.py:108
  111.3 7.9 %copy-start.3 = (bf16[16,2,32,1536]{3,2,1,0:T(8,128)(2,1)}, bf16[16,2,32,1536]{3,2,1,0:T(8,128)(2,1)S(1)}, u32[]{:S(2)}) copy-start(bf16[16,2,32,1536]{3,2,1,0:T(8,128)(2,1)S(1)} %all-to-all-done.2) | copy-start | bytes 9437188
  111.3 7.9 %copy-start.5 = (bf16[16,2,32,1536]{3,2,1,0:T(8,128)(2,1)S(1)}, bf16[16,2,32,1536]{3,2,1,0:T(8,128)(2,1)}, u32[]{:S(2)}) copy-start(bf16[16,2,32,1536]{3,2,1,0:T(8,128)(2,1)} %copy-done.4) | copy-start | bytes 9437188
  119.2 5.4 copy-start.13
  119.2 5.4 copy-start.14
  124.6 5.1 copy-start
  124.6 6.4 copy-start.11
  124.7 6.7 %copy-start.8 = (s32[128,6]{1,0:T(8,128)S(1)}, s32[128,6]{1,0:T(8,128)}, u32[]{:S(2)}) copy-start(s32[128,6]{1,0:T(8,128)} %get-tuple-element.6) | copy-start | bytes 9220
  129.7 102.8 %collective-permute-start = (bf16[1,1536,1536]{2,1,0:T(8,128)(2,1)}, bf16[1,1536,1536]{2,1,0:T(8,128)(2,1)}, u32[]{:S(2)}, u32[]{:S(2)}) collective-permute-start(bf16[1,1536,1536]{2,1,0:T(8,128)(2,1)} %constant_dynamic-slice_fusion.1), channel_id=1, source_target_pairs={{0,16},{16,0},{32,48},{48,32},{64,80},{80,64},{96,112},{112,96},{1... | collective-permute-start | bytes 14155784 | tf_op jit(solution)/shard_map/ppermute | solution.py:10
  142.2 95.9 %all-to-all-start.4 = ((bf16[16,2,32,1536]{3,2,1,0:T(8,128)(2,1)}), bf16[16,2,32,1536]{3,2,1,0:T(8,128)(2,1)S(1)}, u32[]{:S(2)}, u32[]{:S(2)}) async-start(bf16[16,2,32,1536]{3,2,1,0:T(8,128)(2,1)} %copy.44), calls=%async_computation.4 | async-start | bytes 6291456 | tf_op jit(solution)/shard_map/all_to_all | solution.py:113
  153.4 2.1 copy-start.2
  157.1 125.9 %collective-permute-start.3 = (bf16[1,768,1536]{2,1,0:T(8,128)(2,1)}, bf16[1,768,1536]{2,1,0:T(8,128)(2,1)}, u32[]{:S(2)}, u32[]{:S(2)}) collective-permute-start(bf16[1,768,1536]{2,1,0:T(8,128)(2,1)} %constant_dynamic-slice_fusion), channel_id=1, source_target_pairs={{0,16},{16,0},{32,48},{48,32},{64,80},{80,64},{96,112},{112,96},{1... | collective-permute-start | bytes 7077896 | tf_op jit(solution)/shard_map/ppermute | solution.py:10
  232.5 207.1 %collective-permute-start.1 = (bf16[1,1536,1536]{2,1,0:T(8,128)(2,1)}, bf16[1,1536,1536]{2,1,0:T(8,128)(2,1)}, u32[]{:S(2)}, u32[]{:S(2)}) collective-permute-start(bf16[1,1536,1536]{2,1,0:T(8,128)(2,1)} %collective-permute-done), channel_id=1, source_target_pairs={{0,32},{16,48},{32,0},{48,16},{64,96},{80,112},{96,64},{112,80},{1... | collective-permute-start | bytes 14155784 | tf_op jit(solution)/shard_map/ppermute | solution.py:10
  246.8 4.7 copy-start.1
  246.8 4.8 copy-start.9
  246.8 5.0 copy-start.6
  264.3 176.1 %all-to-all-start = ((bf16[16,2,32,1536]{3,2,1,0:T(8,128)(2,1)}), bf16[16,2,32,1536]{3,2,1,0:T(8,128)(2,1)S(1)}, u32[]{:S(2)}, u32[]{:S(2)}) async-start(bf16[16,2,32,1536]{3,2,1,0:T(8,128)(2,1)} %bitcast.1), calls=%async_computation | async-start | bytes 6291456 | tf_op jit(solution)/shard_map/all_to_all | solution.py:105
  283.0 154.1 %collective-permute-start.4 = (bf16[1,768,1536]{2,1,0:T(8,128)(2,1)}, bf16[1,768,1536]{2,1,0:T(8,128)(2,1)}, u32[]{:S(2)}, u32[]{:S(2)}) collective-permute-start(bf16[1,768,1536]{2,1,0:T(8,128)(2,1)} %collective-permute-done.3), channel_id=1, source_target_pairs={{0,32},{16,48},{32,0},{48,16},{64,96},{80,112},{96,64},{112,80},{1... | collective-permute-start | bytes 7077896 | tf_op jit(solution)/shard_map/ppermute | solution.py:10
  437.2 52.8 %collective-permute-start.5 = (bf16[1,768,1536]{2,1,0:T(8,128)(2,1)}, bf16[1,768,1536]{2,1,0:T(8,128)(2,1)}, u32[]{:S(2)}, u32[]{:S(2)}) collective-permute-start(bf16[1,768,1536]{2,1,0:T(8,128)(2,1)} %collective-permute-done.4), channel_id=1, source_target_pairs={{0,64},{16,80},{32,96},{48,112},{64,0},{80,16},{96,32},{112,48},{1... | collective-permute-start | bytes 7077896 | tf_op jit(solution)/shard_map/ppermute | solution.py:10
  439.6 199.8 %collective-permute-start.2 = (bf16[1,1536,1536]{2,1,0:T(8,128)(2,1)}, bf16[1,1536,1536]{2,1,0:T(8,128)(2,1)}, u32[]{:S(2)}, u32[]{:S(2)}) collective-permute-start(bf16[1,1536,1536]{2,1,0:T(8,128)(2,1)} %collective-permute-done.1), channel_id=1, source_target_pairs={{0,64},{16,80},{32,96},{48,112},{64,0},{80,16},{96,32},{112,48},{1... | collective-permute-start | bytes 14155784 | tf_op jit(solution)/shard_map/ppermute | solution.py:10
  455.1 6.0 copy-start.12
  455.1 169.7 %all-to-all-start.1 = ((bf16[16,2,32,1536]{3,2,1,0:T(8,128)(2,1)}), bf16[16,2,32,1536]{3,2,1,0:T(8,128)(2,1)S(1)}, u32[]{:S(2)}, u32[]{:S(2)}) async-start(bf16[16,2,32,1536]{3,2,1,0:T(8,128)(2,1)} %copy.35), calls=%async_computation.1 | async-start | bytes 6291456 | tf_op jit(solution)/shard_map/all_to_all | solution.py:111
where the time goes:
time: 654 us; the launch traced here: 647 us
  waiting for transfers between devices  438 us (67%)
  local copies, waits for them, and re-layouts  69.4 us (11%)
  matrix products  52.2 us (8%)
  other arithmetic  44.8 us (7%)
  starting transfers between devices  41.5 us (6%)
    ppermute x6, waiting for transfers between devices, from_partner(): lax.ppermute(value, axis, [(i, i ^ 1 << bit) for i in range(lax.axis_size...  267 us
    all_to_all x1, waiting for transfers between devices, per_device(): lax.all_to_all(out_fwd, 'expert', split_axis=0, concat_axis=0, tiled=True)  130 us
    all_to_all x1, waiting for transfers between devices, per_device(): lax.all_to_all(send_cot, 'expert', split_axis=0, concat_axis=0, tiled=True)  27.2 us
    scatter x2, local copies, waits for them, and re-layouts, place_rows(): return jnp.zeros((slot_total, values.shape[-1]), values.dtype).at[dest.re...  17.7 us
    scatter x1, other arithmetic, place_rows(): return jnp.zeros((slot_total, values.shape[-1]), values.dtype).at[dest.re...  13.3 us
    all_to_all x1, waiting for transfers between devices, per_device(): lax.all_to_all(send_inputs, 'expert', split_axis=0, concat_axis=0, tiled=...  13.3 us
  transfers between devices with their start and end apart: 11, of which 7 were waited for; matrix products, arithmetic and copies ran while one was open for 18% of the time, Pallas kernels for 0%

commit v1 on v0

v1 whole, which is shorter than its diff:
```python
import jax
import jax.numpy as jnp
from jax import lax
from jax.sharding import PartitionSpec as P

norm_eps = 1e-06
bf16 = jnp.bfloat16
f32 = jnp.float32


def normalize(inputs):
    values = inputs.astype(f32)
    scale = lax.rsqrt(jnp.mean(values * values, axis=-1, keepdims=True) + norm_eps)
    return values * scale, scale


def dispatch_table(routes, gates, expert_count, capacity):
    names = routes[:, :, None] == jnp.arange(expert_count, dtype=jnp.int32)[None, None, :]
    chosen = jnp.any(names, axis=1)
    gate = jnp.sum(jnp.where(names, gates[:, :, None], 0.0), axis=1)
    tokens = routes.shape[0]
    earlier = jnp.tri(tokens, tokens, -1, dtype=bf16)
    slot = jnp.dot(earlier, chosen.astype(bf16), preferred_element_type=f32).astype(jnp.int32)
    slot = jnp.where(chosen, slot, -1)
    pick = slot.T[:, None, :] == jnp.arange(capacity, dtype=jnp.int32)[None, :, None]
    slot_gate = jnp.sum(jnp.where(pick, gate.T[:, None, :], 0.0), axis=-1)
    return pick.astype(bf16), slot_gate


def per_device(
    x_fwd, gate_fwd, route_fwd, x_bwd, gate_bwd, route_bwd, cotangent, norm_gain, w_gate_up, w_down
):
    group_count = lax.axis_size("expert")
    section_count = lax.axis_size("pipe")
    local_count = w_gate_up.shape[1]
    expert_count = local_count * group_count
    token_count, width = x_fwd.shape
    picks = route_fwd.shape[1]
    capacity = token_count * picks * 4 // (3 * expert_count)
    hidden_units = w_down.shape[2]
    section = lax.axis_index("pipe")
    upper = (section >= section_count // 2).astype(jnp.int32)
    weight_gu, weight_dn = w_gate_up[0], w_down[0]

    bwd_hat, bwd_scale = normalize(x_bwd)
    bwd_normed = (bwd_hat * norm_gain).astype(bf16)
    pick_b, slot_gate_b = dispatch_table(route_bwd, gate_bwd, expert_count, capacity)
    order = (2, group_count * capacity)

    def by_parity(pick):
        return (
            pick.reshape(group_count, local_count, capacity, token_count)
            .transpose(1, 0, 2, 3)
            .reshape(expert_count * capacity, token_count)
        )

    pick_bp = by_parity(pick_b)
    gate_bp = (
        slot_gate_b.reshape(group_count, local_count, capacity)
        .transpose(1, 0, 2)
        .reshape(expert_count * capacity)
    )
    send_h = jnp.dot(pick_bp, bwd_normed, preferred_element_type=f32).astype(bf16)
    send_c = (jnp.dot(pick_bp, cotangent, preferred_element_type=f32) * gate_bp[:, None]).astype(bf16)

    pairs = [
        [p * group_count + d for p in (low, section_count - 1 - low) for d in range(group_count)]
        for low in range(section_count // 2)
    ]

    def exchange_pair(value):
        value = value.reshape(expert_count, capacity, width)
        return lax.all_to_all(
            value, ("pipe", "expert"), split_axis=0, concat_axis=0, axis_index_groups=pairs, tiled=True
        )

    def exchange(value):
        return lax.all_to_all(value, "expert", split_axis=0, concat_axis=0, tiled=True)

    recv_h = exchange_pair(send_h).reshape(expert_count * capacity, width)
    recv_c = exchange_pair(send_c).reshape(expert_count * capacity, width)

    fwd_normed = (normalize(x_fwd)[0] * norm_gain).astype(bf16)
    pick_f, slot_gate_f = dispatch_table(route_fwd, gate_fwd, expert_count, capacity)
    pick_f = pick_f.reshape(expert_count * capacity, token_count)
    send_f = jnp.dot(pick_f, fwd_normed, preferred_element_type=f32).astype(bf16)
    recv_f = exchange(send_f.reshape(group_count, local_count, capacity, width))

    own_gu = lax.dynamic_index_in_dim(weight_gu, upper, 0, keepdims=False)
    own_dn = lax.dynamic_index_in_dim(weight_dn, upper, 0, keepdims=False)
    both = jnp.dot(recv_h, own_gu, preferred_element_type=f32)
    gate_pre, up_pre = both[:, :hidden_units], both[:, hidden_units:]
    squash = jax.nn.sigmoid(gate_pre)
    activated = gate_pre * squash
    hidden = (activated * up_pre).astype(bf16)
    back_hidden = lax.dot_general(
        recv_c, own_dn, (((1,), (1,)), ((), ())), preferred_element_type=f32
    )
    d_gate = back_hidden * up_pre * squash * (1.0 + gate_pre * (1.0 - squash))
    d_up = back_hidden * activated
    d_both = jnp.concatenate([d_gate, d_up], axis=-1).astype(bf16)
    d_inputs = lax.dot_general(
        d_both, own_gu, (((1,), (1,)), ((), ())), preferred_element_type=f32
    ).astype(bf16)
    back_dh = exchange_pair(d_inputs).reshape(expert_count * capacity, width)
    grad_dn = lax.dot_general(
        hidden, recv_c, (((0,), (0,)), ((), ())), preferred_element_type=f32
    ).astype(bf16)
    grad_gu = lax.dot_general(
        recv_h, d_both, (((0,), (0,)), ((), ())), preferred_element_type=f32
    ).astype(bf16)

    fwd_both = jnp.einsum("secd,edf->secf", recv_f, weight_gu, preferred_element_type=f32)
    fwd_hidden = (
        jax.nn.silu(fwd_both[..., :hidden_units]) * fwd_both[..., hidden_units:]
    ).astype(bf16)
    out_fwd = jnp.einsum(
        "secf,efd->secd", fwd_hidden, weight_dn, preferred_element_type=f32
    ).astype(bf16)
    back_fwd = exchange(out_fwd).reshape(expert_count * capacity, width)

    scaled = (back_fwd.astype(f32) * slot_gate_f.reshape(-1)[:, None]).astype(bf16)
    contract_slots = (((0,), (0,)), ((), ()))
    y_fwd = lax.dot_general(pick_f, scaled, contract_slots, preferred_element_type=f32).astype(bf16)
    dh_sum = lax.dot_general(pick_bp, back_dh, contract_slots, preferred_element_type=f32)
    scaled_dh = norm_gain * dh_sum
    dx_bwd = (
        bwd_scale * (scaled_dh - bwd_hat * jnp.mean(bwd_hat * scaled_dh, axis=-1, keepdims=True))
    ).astype(bf16)
    return y_fwd, dx_bwd, grad_gu[None, None], grad_dn[None, None]


def solution(mesh):
    rows = P(("pipe", "expert"), None)
    weights = P("pipe", "expert", None, None)
    return jax.shard_map(
        per_device,
        mesh=mesh,
        in_specs=(rows,) * 7 + (P(), weights, weights),
        out_specs=(rows, rows, weights, weights),
        check_vma=False,
    )
```

time: 654 us -> 255 us (0.39)
  waiting for transfers between devices: 438 us -> 126 us
  local copies, waits for them, and re-layouts: 69.4 us -> 13.2 us
  other arithmetic: 44.8 us -> 8.25 us
  matrix products: 52.2 us -> 68.6 us
  starting transfers between devices: 41.5 us -> 33 us
    ppermute x6 -> x0, waiting for transfers between devices: 267 us -> none  [from_partner(): lax.ppermute(value, axis, [(i, i ^ 1 << bit) for i in range(lax.axis_size...]
    all_to_all x5, waiting for transfers between devices: 171 us -> 126 us  [the longest x3 85.3 us: exchange_pair(): lax.all_to_all(value, ('pipe', 'expert'), split_axis=0, concat_axis=0, ax...]
    scatter x2 -> x0, local copies, waits for them, and re-layouts: 17.7 us -> none  [place_rows(): return jnp.zeros((slot_total, values.shape[-1]), values.dtype).at[dest.re...]
    dot_general x7 -> x14, matrix products: 52.2 us -> 68.6 us  [the longest x1 9.2 us: per_device(): lax.dot_general(recv_h, d_both, (((0,), (0,)), ((), ())), preferred_eleme...]
    scatter x1 -> x0, other arithmetic: 13.3 us -> none  [place_rows(): return jnp.zeros((slot_total, values.shape[-1]), values.dtype).at[dest.re...]
    convert_element_type x4 -> x1, local copies, waits for them, and re-layouts: 13.9 us -> 1.99 us  [per_device(): out_fwd = jnp.einsum('secf,efd->secd', fwd_hidden, weight_dn, preferred_e...]
    broadcast_in_dim x2 -> x0, other arithmetic: 11.6 us -> none  [per_device(): return (y_fwd, dx_bwd, out_gu[None], out_dn[None])]
    ppermute x6 -> x0, starting transfers between devices: 10.6 us -> none  [from_partner(): lax.ppermute(value, axis, [(i, i ^ 1 << bit) for i in range(lax.axis_size...]
  transfers between devices with their start and end apart: 11 -> 5, of which waited for: 7 -> 5; matrix products, arithmetic and copies ran while one was open for 18% -> 29% of each run, Pallas kernels for 0% -> 0%
where the time goes in v1:
time: 255 us; the launch traced here: 250 us
  waiting for transfers between devices  126 us (49%)
  matrix products  68.6 us (27%)
  starting transfers between devices  33 us (13%)
  local copies, waits for them, and re-layouts  13.2 us (5%)
  other arithmetic  8.25 us (3%)
    all_to_all x3, waiting for transfers between devices, exchange_pair(): lax.all_to_all(value, ('pipe', 'expert'), split_axis=0, concat_axis=0, ax...  85.3 us
    all_to_all x2, waiting for transfers between devices, exchange(): lax.all_to_all(value, 'expert', split_axis=0, concat_axis=0, tiled=True)  40.9 us
    all_to_all x3, starting transfers between devices, exchange_pair(): lax.all_to_all(value, ('pipe', 'expert'), split_axis=0, concat_axis=0, ax...  20 us
    all_to_all x2, starting transfers between devices, exchange(): lax.all_to_all(value, 'expert', split_axis=0, concat_axis=0, tiled=True)  13.1 us
    dot_general x1, matrix products, per_device(): lax.dot_general(recv_h, d_both, (((0,), (0,)), ((), ())), preferred_eleme...  9.2 us
    dot_general x1, matrix products, per_device(): jnp.einsum('secd,edf->secf', recv_f, weight_gu, preferred_element_type=f32)  8.53 us
    dot_general x1, matrix products, per_device(): both = jnp.dot(recv_h, own_gu, preferred_element_type=f32)  8.28 us
    dot_general x1, matrix products, per_device(): lax.dot_general(hidden, recv_c, (((0,), (0,)), ((), ())), preferred_eleme...  7.93 us
  transfers between devices with their start and end apart: 5, of which 5 were waited for; matrix products, arithmetic and copies ran while one was open for 29% of the time, Pallas kernels for 0%

profile of v1, /device:TPU:1, one launch (start us, length us, event | category | flops | bytes accessed | tf_op | source)
XLA Modules:
  0.0 250.2 jit_solution(1474920744448147562)
XLA Ops:
  0.6 0.0 copy-start
  0.7 0.0 copy-start.16
  0.7 1.2 fusion.37
  1.9 0.7 fusion.54
  2.6 0.1 eq.111
  2.7 0.2 fusion.33
  2.9 0.2 bitcast_compare_fusion.1
  3.1 3.7 %convolution_convert_fusion.2 = bf16[1024,1536]{1,0:T(8,128)(2,1)} fusion(pred[1024,128]{1,0:T(32,128)(4,1)S(1)} %bitcast_compare_fusion.1, bf16[128,1536]{1,0:T(8,128)(2,1)} %param.10, f32[1536]{0:T(1024)} %param.17, f32[128]{0:T(128)S(1)} %add_rsqrt_fusion.1), kind=kOutput, calls=%fused_computation.18 | convolution fusion | flops 405012480 | bytes 3676672 | tf_op jit(solution)/shard_map/dot_general | solution.py:86
  6.8 7.8 %all-to-all-start = ((bf16[16,2,32,1536]{3,2,1,0:T(8,128)(2,1)}), bf16[16,2,32,1536]{3,2,1,0:T(8,128)(2,1)S(1)}, u32[]{:S(2)}, u32[]{:S(2)}) async-start(bf16[16,2,32,1536]{3,2,1,0:T(8,128)(2,1)} %bitcast.3), calls=%async_computation | async-start | bytes 6291456 | tf_op jit(solution)/shard_map/all_to_all | solution.py:78
  14.6 0.7 fusion.53
  15.3 0.9 fusion.32
  16.2 0.6 copy.55
  16.8 0.7 select_reduce_fusion.2
  17.5 0.2 select_reduce_fusion
  17.8 0.6 copy.56
  18.4 1.4 mul.120
  19.7 0.6 eq.124
  20.3 1.4 eq.125
  21.7 0.9 bitcast_compare_fusion
  22.7 0.0 copy-start.7
  22.7 0.6 copy-done.7
  23.3 3.3 %multiply_convert_fusion = bf16[1024,1536]{1,0:T(8,128)(2,1)} fusion(pred[1024,128]{1,0:T(32,128)(4,1)S(1)} %bitcast_compare_fusion, bf16[128,1536]{1,0:T(8,128)(2,1)S(1)} %copy-done, f32[1024]{0:T(1024)} %mul.120), kind=kOutput, calls=%fused_computation.4 | convolution fusion | flops 405798912 | bytes 3674112 | tf_op jit(solution)/shard_map/dot_general | solution.py:64
  26.6 26.3 %all-to-all-done = bf16[16,2,32,1536]{3,2,1,0:T(8,128)(2,1)S(1)} async-done(((bf16[16,2,32,1536]{3,2,1,0:T(8,128)(2,1)}), bf16[16,2,32,1536]{3,2,1,0:T(8,128)(2,1)S(1)}, u32[]{:S(2)}, u32[]{:S(2)}) %all-to-all-start) | async-done | bytes 3145760 | tf_op jit(solution)/shard_map/all_to_all | solution.py:78
  52.9 1.7 copy-done.6
  54.6 8.4 %all-to-all-start.2 = ((bf16[32,32,1536]{2,1,0:T(8,128)(2,1)}), bf16[32,32,1536]{2,1,0:T(8,128)(2,1)S(1)}, u32[]{:S(2)}, u32[]{:S(2)}) async-start(bf16[32,32,1536]{2,1,0:T(8,128)(2,1)} %bitcast.23), calls=%async_computation.2 | async-start | bytes 6291456 | tf_op jit(solution)/shard_map/all_to_all | solution.py:73
  63.1 0.2 fusion.45
  63.2 0.5 copy-done.13
  63.8 3.6 %convolution_convert_fusion.1 = bf16[1024,1536]{1,0:T(8,128)(2,1)} fusion(pred[1024,128]{1,0:T(32,128)(4,1)} %copy-done.7, bf16[128,1536]{1,0:T(8,128)(2,1)S(1)} %copy-done.2, f32[128]{0:T(128)S(1)} %add_rsqrt_fusion, f32[1536]{0:T(1024)} %param.17), kind=kOutput, calls=%fused_computation.17 | convolution fusion | flops 405012480 | bytes 3676672 | tf_op jit(solution)/shard_map/dot_general | solution.py:63
  67.4 37.3 %all-to-all-done.2 = bf16[32,32,1536]{2,1,0:T(8,128)(2,1)S(1)} async-done(((bf16[32,32,1536]{2,1,0:T(8,128)(2,1)}), bf16[32,32,1536]{2,1,0:T(8,128)(2,1)S(1)}, u32[]{:S(2)}, u32[]{:S(2)}) %all-to-all-start.2) | async-done | bytes 3145760 | tf_op jit(solution)/shard_map/all_to_all | solution.py:73
  104.7 1.6 copy-done.4
  106.3 6.2 %all-to-all-start.3 = ((bf16[32,32,1536]{2,1,0:T(8,128)(2,1)}), bf16[32,32,1536]{2,1,0:T(8,128)(2,1)}, u32[]{:S(2)}, u32[]{:S(2)}) async-start(bf16[32,32,1536]{2,1,0:T(8,128)(2,1)} %bitcast.26), calls=%async_computation.3 | async-start | bytes 6291456 | tf_op jit(solution)/shard_map/all_to_all | solution.py:73
  112.6 0.2 select_reduce_fusion.1
  112.9 0.7 iota_compare_fusion.1
  113.6 0.7 iota_compare_fusion.2
  114.3 8.5 %fusion.9 = f32[16,2,32,1536]{3,2,0,1:T(8,128)S(1)} fusion(bf16[1,2,1536,1536]{3,2,1,0:T(8,128)(2,1)} %param.18, bf16[16,2,32,1536]{3,2,1,0:T(8,128)(2,1)} %copy-done.6), kind=kOutput, calls=%fused_computation.12 | convolution fusion | flops 4831838208 | bytes 18874368 | tf_op jit(solution)/shard_map/secd,edf->secf/dot_general | solution.py:113
  122.9 5.2 %fusion.20 = bf16[16,2,32,1536]{3,2,0,1:T(8,128)(2,1)S(1)} fusion(bf16[1,2,768,1536]{3,2,1,0:T(8,128)(2,1)} %param.19, f32[16,2,32,1536]{3,2,0,1:T(8,128)S(1)} %fusion.9), kind=kOutput, calls=%fused_computation.20 | convolution fusion | flops 2422210560 | bytes 14155776 | tf_op jit(solution)/shard_map/secf,efd->secd/dot_general | solution.py:117
  128.1 2.0 copy.54
  130.1 24.2 %all-to-all-done.3 = bf16[32,32,1536]{2,1,0:T(8,128)(2,1)} async-done(((bf16[32,32,1536]{2,1,0:T(8,128)(2,1)}), bf16[32,32,1536]{2,1,0:T(8,128)(2,1)}, u32[]{:S(2)}, u32[]{:S(2)}) %all-to-all-start.3) | async-done | bytes 3145760 | tf_op jit(solution)/shard_map/all_to_all | solution.py:73
  154.3 5.3 %all-to-all-start.1 = ((bf16[16,2,32,1536]{3,2,1,0:T(8,128)(2,1)}), bf16[16,2,32,1536]{3,2,1,0:T(8,128)(2,1)S(1)}, u32[]{:S(2)}, u32[]{:S(2)}) async-start(bf16[16,2,32,1536]{3,2,1,0:T(8,128)(2,1)} %copy.54), calls=%async_computation.1 | async-start | bytes 6291456 | tf_op jit(solution)/shard_map/all_to_all | solution.py:78
  159.6 0.0 slice-start
  159.6 0.0 slice-start.1
  159.6 8.3 %fusion.7 = f32[1024,1536]{0,1:T(8,128)S(1)} fusion(bf16[1024,1536]{1,0:T(8,128)(2,1)} %bitcast.27, bf16[1,2,1536,1536]{3,2,1,0:T(8,128)(2,1)} %param.18, s32[]{:T(128)S(6)} %select_n.35), kind=kOutput, calls=%fused_computation.10 | convolution fusion | flops 4831838208 | bytes 14155780 | tf_op jit(solution)/shard_map/dot_general | solution.py:91
  167.9 0.0 copy-start.17
  167.9 0.0 copy-done.5
  167.9 0.0 slice-start.2
  167.9 7.1 %multiply_convert_fusion.4 = (bf16[1024,768]{0,1:T(8,128)(2,1)S(1)}, bf16[1024,768]{0,1:T(8,128)(2,1)S(1)}) fusion(f32[1024,1536]{0,1:T(8,128)S(1)} %fusion.7, bf16[1024,1536]{1,0:T(8,128)(2,1)S(1)} %bitcast.81, bf16[1,2,768,1536]{3,2,1,0:T(8,128)(2,1)} %param.19, s32[]{:T(128)S(6)} %select_n.35), kind=kOutput, calls=%fused_computation.27 | convolution fusion | flops 2426142720 | bytes 14942212 | tf_op jit(solution)/shard_map/dot_general | solution.py:96
  175.1 1.1 copy-done.18
  176.2 0.5 copy-done.20
  176.7 0.0 slice-done.2
  176.7 6.7 %fusion.14 = bf16[1024,1536]{1,0:T(8,128)(2,1)} fusion(bf16[1,2,1536,1536]{3,2,1,0:T(8,128)(2,1)S(1)} %bitcast.91, s32[]{:T(128)S(6)} %select_n.35, bf16[1024,768]{0,1:T(8,128)(2,1)S(1)} %get-tuple-element.5, bf16[1024,768]{0,1:T(8,128)(2,1)S(1)} %get-tuple-element.4), kind=kOutput, calls=%fused_computation.15 | convolution fusion | flops 4839702528 | bytes 11010052 | tf_op jit(solution)/shard_map/dot_general | solution.py:102
  183.4 14.5 %all-to-all-done.1 = bf16[16,2,32,1536]{3,2,1,0:T(8,128)(2,1)S(1)} async-done(((bf16[16,2,32,1536]{3,2,1,0:T(8,128)(2,1)}), bf16[16,2,32,1536]{3,2,1,0:T(8,128)(2,1)S(1)}, u32[]{:S(2)}, u32[]{:S(2)}) %all-to-all-start.1) | async-done | bytes 3145760 | tf_op jit(solution)/shard_map/all_to_all | solution.py:78
  197.9 5.3 %all-to-all-start.4 = ((bf16[32,32,1536]{2,1,0:T(8,128)(2,1)}), bf16[32,32,1536]{2,1,0:T(8,128)(2,1)}, u32[]{:S(2)}, u32[]{:S(2)}) async-start(bf16[32,32,1536]{2,1,0:T(8,128)(2,1)} %bitcast.82), calls=%async_computation.4 | async-start | bytes 6291456 | tf_op jit(solution)/shard_map/all_to_all | solution.py:73
  203.2 0.0 copy-start.19
  203.2 0.0 copy-start.21
  203.2 7.9 %fusion.26 = bf16[1,1,768,1536]{3,2,1,0:T(8,128)(2,1)} fusion(bf16[1024,1536]{1,0:T(8,128)(2,1)} %bitcast.80, f32[1024,1536]{0,1:T(8,128)} %copy-done.17), kind=kOutput, calls=%fused_computation.30 | convolution fusion | flops 2421817344 | bytes 11796480 | tf_op jit(solution)/shard_map/dot_general | solution.py:106
  211.2 9.2 %fusion.2 = bf16[1,1,1536,1536]{3,2,1,0:T(8,128)(2,1)} fusion(bf16[1024,1536]{1,0:T(8,128)(2,1)} %bitcast.27, bf16[1024,768]{0,1:T(8,128)(2,1)S(1)} %copy-done.21, bf16[1024,768]{0,1:T(8,128)(2,1)S(1)} %copy-done.19), kind=kOutput, calls=%fused_computation.3 | convolution fusion | flops 4840488960 | bytes 11010048 | tf_op jit(solution)/shard_map/dot_general | solution.py:109
  220.4 0.6 multiply_convert_fusion.1
  220.9 0.0 copy-start.3
  221.0 0.0 copy-start.11
  221.0 0.3 copy-done.9
  221.3 1.4 convolution_convert_fusion.4
  222.6 23.9 %all-to-all-done.4 = bf16[32,32,1536]{2,1,0:T(8,128)(2,1)} async-done(((bf16[32,32,1536]{2,1,0:T(8,128)(2,1)}), bf16[32,32,1536]{2,1,0:T(8,128)(2,1)}, u32[]{:S(2)}, u32[]{:S(2)}) %all-to-all-start.4) | async-done | bytes 3145760 | tf_op jit(solution)/shard_map/all_to_all | solution.py:73
  246.5 2.6 %fusion.41 = (f32[128]{0:T(128)S(1)}, f32[128,1536]{1,0:T(8,128)S(1)}) fusion(bf16[128,1536]{1,0:T(8,128)(2,1)S(1)} %copy-done.3, f32[128]{0:T(128)S(1)} %copy-done.14, pred[1024,128]{1,0:T(32,128)(4,1)S(1)} %bitcast.83, bf16[1024,1536]{1,0:T(8,128)(2,1)} %bitcast.30, f32[1536]{0:T(1024)S(1)} %copy-done.11), kind=kOutput, calls=%fused_computation.52 | convolution fusion | flops 403636096 | bytes 4463616 | tf_op jit(solution)/shard_map/dot_general | solution.py:125
  249.2 1.0 fusion.44
  (37 shorter events, 0.1 us)
Async XLA Ops:
  0.6 22.7 %copy-start = (bf16[128,1536]{1,0:T(8,128)(2,1)S(1)}, bf16[128,1536]{1,0:T(8,128)(2,1)}, u32[]{:S(2)}) copy-start(bf16[128,1536]{1,0:T(8,128)(2,1)} %param.16) | copy-start | bytes 1179652
  0.7 6.2 %copy-start.16 = (s32[128]{0:T(128)}, s32[128]{0:T(128)S(1)}, u32[]{:S(2)}) copy-start(s32[128]{0:T(128)S(1)} %iota_add_fusion) | copy-start | bytes 1540
  6.8 46.1 %all-to-all-start = ((bf16[16,2,32,1536]{3,2,1,0:T(8,128)(2,1)}), bf16[16,2,32,1536]{3,2,1,0:T(8,128)(2,1)S(1)}, u32[]{:S(2)}, u32[]{:S(2)}) async-start(bf16[16,2,32,1536]{3,2,1,0:T(8,128)(2,1)} %bitcast.3), calls=%async_computation | async-start | bytes 6291456 | tf_op jit(solution)/shard_map/all_to_all | solution.py:78
  22.7 0.7 copy-start.7
  52.9 1.7 copy-start.6
  52.9 10.1 %copy-start.2 = (bf16[128,1536]{1,0:T(8,128)(2,1)S(1)}, bf16[128,1536]{1,0:T(8,128)(2,1)}, u32[]{:S(2)}) copy-start(bf16[128,1536]{1,0:T(8,128)(2,1)} %param.13) | copy-start | bytes 1179652
  54.6 50.1 %all-to-all-start.2 = ((bf16[32,32,1536]{2,1,0:T(8,128)(2,1)}), bf16[32,32,1536]{2,1,0:T(8,128)(2,1)S(1)}, u32[]{:S(2)}, u32[]{:S(2)}) async-start(bf16[32,32,1536]{2,1,0:T(8,128)(2,1)} %bitcast.23), calls=%async_computation.2 | async-start | bytes 6291456 | tf_op jit(solution)/shard_map/all_to_all | solution.py:73
  63.2 0.5 copy-start.13
  104.7 1.6 copy-start.4
  104.7 7.9 %copy-start.12 = (s32[128,6]{0,1:T(8,128)S(1)}, s32[128,6]{0,1:T(8,128)}, u32[]{:S(2)}) copy-start(s32[128,6]{0,1:T(8,128)} %param.12) | copy-start | bytes 9220
  104.7 7.9 %copy-start.15 = (f32[128,6]{0,1:T(8,128)S(1)}, f32[128,6]{0,1:T(8,128)}, u32[]{:S(2)}) copy-start(f32[128,6]{0,1:T(8,128)} %param.11) | copy-start | bytes 9220
  104.7 8.2 %copy-start.10 = (s32[2,16,128]{2,1,0:T(8,128)S(1)}, s32[2,16,128]{2,1,0:T(8,128)}, u32[]{:S(2)}) copy-start(s32[2,16,128]{2,1,0:T(8,128)} %copy.55) | copy-start | bytes 49156
  106.3 47.9 %all-to-all-start.3 = ((bf16[32,32,1536]{2,1,0:T(8,128)(2,1)}), bf16[32,32,1536]{2,1,0:T(8,128)(2,1)}, u32[]{:S(2)}, u32[]{:S(2)}) async-start(bf16[32,32,1536]{2,1,0:T(8,128)(2,1)} %bitcast.26), calls=%async_computation.3 | async-start | bytes 6291456 | tf_op jit(solution)/shard_map/all_to_all | solution.py:73
  154.3 43.6 %all-to-all-start.1 = ((bf16[16,2,32,1536]{3,2,1,0:T(8,128)(2,1)}), bf16[16,2,32,1536]{3,2,1,0:T(8,128)(2,1)S(1)}, u32[]{:S(2)}, u32[]{:S(2)}) async-start(bf16[16,2,32,1536]{3,2,1,0:T(8,128)(2,1)} %copy.54), calls=%async_computation.1 | async-start | bytes 6291456 | tf_op jit(solution)/shard_map/all_to_all | solution.py:78
  159.6 8.3 %copy-start.5 = (bf16[32,32,1536]{2,1,0:T(8,128)(2,1)S(1)}, bf16[32,32,1536]{2,1,0:T(8,128)(2,1)}, u32[]{:S(2)}) copy-start(bf16[32,32,1536]{2,1,0:T(8,128)(2,1)} %copy-done.4) | copy-start | bytes 9437188
  159.6 17.1 %slice-start = ((s8[9437184]{0:T(1024)(128)(4,1)}), s8[4194304]{0:T(1024)(128)(4,1)S(1)}, s32[]{:S(2)}) async-start(s8[9437184]{0:T(1024)(128)(4,1)} %bitcast.90), calls=%async_computation.5 | async-start | bytes 8388608
  159.6 17.1 %slice-start.1 = ((s8[9437184]{0:T(1024)(128)(4,1)}), s8[4194304]{0:T(1024)(128)(4,1)S(1)}, s32[]{:S(2)}) async-start(s8[9437184]{0:T(1024)(128)(4,1)} %bitcast.90), calls=%async_computation.6 | async-start | bytes 8388608
  167.9 7.2 %copy-start.17 = (f32[1024,1536]{0,1:T(8,128)}, f32[1024,1536]{0,1:T(8,128)S(1)}, u32[]{:S(2)}) copy-start(f32[1024,1536]{0,1:T(8,128)S(1)} %fusion.7) | copy-start | bytes 18874372
  167.9 8.8 %slice-start.2 = ((s8[9437184]{0:T(1024)(128)(4,1)}), s8[1048576]{0:T(1024)(128)(4,1)S(1)}, s32[]{:S(2)}) async-start(s8[9437184]{0:T(1024)(128)(4,1)} %bitcast.90), calls=%async_computation.7 | async-start | bytes 2097152
  175.1 1.2 copy-start.18
  175.1 1.7 copy-start.20
  197.9 48.6 %all-to-all-start.4 = ((bf16[32,32,1536]{2,1,0:T(8,128)(2,1)}), bf16[32,32,1536]{2,1,0:T(8,128)(2,1)}, u32[]{:S(2)}, u32[]{:S(2)}) async-start(bf16[32,32,1536]{2,1,0:T(8,128)(2,1)} %bitcast.82), calls=%async_computation.4 | async-start | bytes 6291456 | tf_op jit(solution)/shard_map/all_to_all | solution.py:73
  203.2 7.9 %copy-start.19 = (bf16[1024,768]{0,1:T(8,128)(2,1)S(1)}, bf16[1024,768]{0,1:T(8,128)(2,1)}, u32[]{:S(2)}) copy-start(bf16[1024,768]{0,1:T(8,128)(2,1)} %copy-done.18) | copy-start | bytes 4718596
  203.2 7.9 %copy-start.21 = (bf16[1024,768]{0,1:T(8,128)(2,1)S(1)}, bf16[1024,768]{0,1:T(8,128)(2,1)}, u32[]{:S(2)}) copy-start(bf16[1024,768]{0,1:T(8,128)(2,1)} %copy-done.20) | copy-start | bytes 4718596
  220.4 0.9 copy-start.9
  220.9 25.6 %copy-start.3 = (bf16[128,1536]{1,0:T(8,128)(2,1)S(1)}, bf16[128,1536]{1,0:T(8,128)(2,1)}, u32[]{:S(2)}) copy-start(bf16[128,1536]{1,0:T(8,128)(2,1)} %param.13) | copy-start | bytes 1179652
  221.0 25.6 %copy-start.8 = (pred[2,16,32,128]{3,2,1,0:T(32,128)(4,1)S(1)}, pred[2,16,32,128]{3,2,1,0:T(32,128)(4,1)}, u32[]{:S(2)}) copy-start(pred[2,16,32,128]{3,2,1,0:T(32,128)(4,1)} %iota_compare_fusion.1) | copy-start | bytes 393220
  221.0 25.6 %copy-start.11 = (f32[1536]{0:T(1024)S(1)}, f32[1536]{0:T(1024)}, u32[]{:S(2)}) copy-start(f32[1536]{0:T(1024)} %param.17) | copy-start | bytes 18436
  221.0 25.5 %copy-start.14 = (f32[128]{0:T(128)S(1)}, f32[128]{0:T(128)}, u32[]{:S(2)}) copy-start(f32[128]{0:T(128)} %copy-done.13) | copy-start | bytes 1540
  221.3 28.9 %copy-start.1 = (bf16[128,1536]{1,0:T(8,128)(2,1)S(1)}, bf16[128,1536]{1,0:T(8,128)(2,1)}, u32[]{:S(2)}) copy-start(bf16[128,1536]{1,0:T(8,128)(2,1)} %param.16) | copy-start | bytes 1179652

commit v2 on v1

v2 whole, which is shorter than its diff:
```python
import functools

import jax
import jax.numpy as jnp
from jax import lax
from jax.experimental import pallas as pl
from jax.experimental.pallas import tpu as pltpu
from jax.sharding import PartitionSpec as P

norm_eps = 1e-06
bf16 = jnp.bfloat16
f32 = jnp.float32
MESH = pl.DeviceIdType.MESH
CAP = 32
TILE = 256
PIECE = 8 * CAP
NT = (((1,), (1,)), ((), ()))


def normalize(inputs):
    values = inputs.astype(f32)
    scale = lax.rsqrt(jnp.mean(values * values, axis=-1, keepdims=True) + norm_eps)
    return values * scale, scale


def place():
    p, d = lax.axis_index("pipe"), lax.axis_index("expert")
    half = p // 4
    return p, half, d // 4, (d // 2) % 2, d % 2


def peer(sign, kz, kx, kc, kh):
    p, half, z, xl, c = place()
    to_half = (half + kh) % 2
    flip = (half + to_half) % 2
    to_p = p + flip * (7 - 2 * p)
    to_z = (z + sign * kz + 4) % 4
    return to_p, to_z * 4 + ((xl + kx) % 2) * 2 + (c + kc) % 2


def dot(a, b):
    return jnp.dot(a, b, preferred_element_type=f32)


def dot_nt(a, b):
    return lax.dot_general(a, b, NT, preferred_element_type=f32)


def kernel(
    send_f, send_h, send_c, w_gu, w_dn,
    back_f, back_dh, grad_gu, grad_dn,
    got_f, got_h, got_c, gu, dn, out_f, out_dh, hid_f, hid, dboth, lhs_t, gout,
    w_sem, own_sem, fs_sem, fr_sem, hs_sem, hr_sem, cs_sem, cr_sem, ds_sem, dr_sem, es_sem, er_sem,
    g_sem,
):
    width = got_h.shape[1]
    units = dn.shape[1]
    p, half, z, xl, c = place()

    own = [
        pltpu.make_async_copy(send_f.at[0, 0], got_f.at[0, pl.ds(0, CAP)], own_sem.at[0]),
        pltpu.make_async_copy(send_f.at[1, 0], got_f.at[1, pl.ds(0, CAP)], own_sem.at[1]),
        pltpu.make_async_copy(send_h.at[0], got_h.at[pl.ds(0, CAP)], own_sem.at[2]),
        pltpu.make_async_copy(send_c.at[0], got_c.at[pl.ds(0, CAP)], own_sem.at[3]),
    ]
    weights = [
        pltpu.make_async_copy(w_gu, gu, w_sem.at[0]),
        pltpu.make_async_copy(w_dn, dn, w_sem.at[1]),
    ]
    for copy in own + weights:
        copy.start()

    barrier = pltpu.get_barrier_semaphore()

    def greet(k, _):
        to = peer(1, k % 4, (k // 8) % 2, (k // 4) % 2, k // 16)
        pl.semaphore_signal(barrier, inc=1, device_id=to, device_id_type=MESH)
        return 0

    lax.fori_loop(1, 32, greet, 0)
    pl.semaphore_wait(barrier, 31)

    def remote(src, dst, ssem, rsem, to):
        return pltpu.make_async_remote_copy(
            src_ref=src, dst_ref=dst, send_sem=ssem, recv_sem=rsem, device_id=to, device_id_type=MESH
        )

    def send_fwd(a):
        def go(j, _):
            to = peer(1, j % 4, a, j // 4, 0)
            slot = a * 8 + j
            rows = pl.ds(slot * CAP, CAP)
            for e in range(2):
                remote(
                    send_f.at[e, slot], got_f.at[e, rows], fs_sem.at[a, e], fr_sem.at[a, e], to
                ).start()
            return 0

        lax.fori_loop(1 if a == 0 else 0, 8, go, 0)

    def send_bwd(q):
        def go(j, _):
            to = peer(1, j % 4, q // 2, q % 2, j // 4)
            slot = q * 8 + j
            rows = pl.ds(slot * CAP, CAP)
            remote(send_h.at[slot], got_h.at[rows], hs_sem.at[q], hr_sem.at[q], to).start()
            remote(send_c.at[slot], got_c.at[rows], cs_sem.at[q], cr_sem.at[q], to).start()
            return 0

        lax.fori_loop(1 if q == 0 else 0, 8, go, 0)

    def return_fwd(a, e):
        def go(j, _):
            to = peer(-1, j % 4, a, j // 4, 0)
            slot = a * 8 + j
            remote(
                out_f.at[e, pl.ds(slot * CAP, CAP)], back_f.at[e, slot],
                ds_sem.at[e], dr_sem.at[e], to,
            ).start()
            return 0

        lax.fori_loop(1 if a == 0 else 0, 8, go, 0)

    def return_bwd(q):
        def go(j, _):
            to = peer(-1, j % 4, q // 2, q % 2, j // 4)
            slot = q * 8 + j
            remote(
                out_dh.at[pl.ds(slot * CAP, CAP)], back_dh.at[slot], es_sem.at[0], er_sem.at[0], to
            ).start()
            return 0

        lax.fori_loop(1 if q == 0 else 0, 8, go, 0)

    def span(q):
        first = CAP if q == 0 else 0
        return pl.ds(q * PIECE + first, PIECE - first)

    def landed(dst, ssem, rsem):
        return remote(dst, dst, ssem, rsem, (p, d_self))

    d_self = z * 4 + xl * 2 + c

    send_fwd(0)
    send_fwd(1)
    send_bwd(0)

    def forward_piece(a, e):
        rows = pl.ds(a * PIECE, PIECE)

        def first(t, _):
            at = pl.multiple_of(t * TILE, TILE)
            x = got_f[e, rows, :]
            gate = dot(x, gu[e, :, pl.ds(at, TILE)])
            up = dot(x, gu[e, :, pl.ds(units + at, TILE)])
            hid_f[:, pl.ds(at, TILE)] = (gate * jax.nn.sigmoid(gate) * up).astype(bf16)
            return 0

        lax.fori_loop(0, units // TILE, first, 0)

        def second(t, _):
            cols = pl.ds(pl.multiple_of(t * TILE, TILE), TILE)
            out_f[e, rows, cols] = dot(hid_f[...], dn[e, :, cols]).astype(bf16)
            return 0

        lax.fori_loop(0, width // TILE, second, 0)

    def backward_chain(q):
        rows = pl.ds(q * PIECE, PIECE)

        def first(t, _):
            at = pl.multiple_of(t * TILE, TILE)
            cols = pl.ds(at, TILE)
            more = pl.ds(units + at, TILE)
            x = got_h[rows, :]
            gate = dot(x, gu[half, :, cols])
            up = dot(x, gu[half, :, more])
            back = dot_nt(got_c[rows, :], dn[half, cols, :])
            squash = jax.nn.sigmoid(gate)
            active = gate * squash
            hid[rows, cols] = (active * up).astype(bf16)
            dboth[rows, cols] = (back * up * squash * (1.0 + gate * (1.0 - squash))).astype(bf16)
            dboth[rows, more] = (back * active).astype(bf16)
            return 0

        lax.fori_loop(0, units // TILE, first, 0)

        def second(t, _):
            cols = pl.ds(pl.multiple_of(t * TILE, TILE), TILE)
            out_dh[rows, cols] = dot_nt(dboth[rows, :], gu[half, cols, :]).astype(bf16)
            return 0

        lax.fori_loop(0, width // TILE, second, 0)

    for copy in own + weights:
        copy.wait()
    for a in range(2):
        for e in range(2):
            landed(got_f.at[e, span(a)], fs_sem.at[a, e], fr_sem.at[a, e]).wait_recv()
        send_bwd(1 + a)
        for e in range(2):
            forward_piece(a, e)
            return_fwd(a, e)
    send_bwd(3)
    for q in range(4):
        landed(got_h.at[span(q)], hs_sem.at[q], hr_sem.at[q]).wait_recv()
        landed(got_c.at[span(q)], cs_sem.at[q], cr_sem.at[q]).wait_recv()
        backward_chain(q)
        return_bwd(q)

    mine = [
        pltpu.make_async_copy(out_f.at[0, pl.ds(0, CAP)], back_f.at[0, 0], own_sem.at[0]),
        pltpu.make_async_copy(out_f.at[1, pl.ds(0, CAP)], back_f.at[1, 0], own_sem.at[1]),
        pltpu.make_async_copy(out_dh.at[pl.ds(0, CAP)], back_dh.at[0], own_sem.at[2]),
    ]
    for copy in mine:
        copy.start()

    def strips(lhs, rhs, count, dst, buf):
        def strip(m, _):
            at = pl.multiple_of(m * TILE, TILE)
            lhs_t[...] = lhs[:, pl.ds(at, TILE)].T

            def cols_of(t, _):
                cols = pl.ds(pl.multiple_of(t * TILE, TILE), TILE)
                gout[buf, :, cols] = dot(lhs_t[...], rhs[:, cols]).astype(bf16)
                return 0

            lax.fori_loop(0, width // TILE, cols_of, 0)
            copy = pltpu.make_async_copy(gout.at[buf], dst.at[pl.ds(at, TILE)], g_sem.at[buf])
            copy.start()
            copy.wait()
            return 0

        lax.fori_loop(0, count, strip, 0)

    strips(got_h, dboth, width // TILE, grad_gu, 0)
    strips(hid, got_c, units // TILE, grad_dn, 1)

    for a in range(2):
        for e in range(2):
            landed(got_f.at[e, span(a)], fs_sem.at[a, e], fr_sem.at[a, e]).wait_send()
    for q in range(4):
        landed(got_h.at[span(q)], hs_sem.at[q], hr_sem.at[q]).wait_send()
        landed(got_c.at[span(q)], cs_sem.at[q], cr_sem.at[q]).wait_send()
    for e in range(2):
        all_f = landed(back_f.at[e, pl.ds(1, 15)], ds_sem.at[e], dr_sem.at[e])
        all_f.wait_send()
        all_f.wait_recv()
    all_dh = landed(back_dh.at[pl.ds(1, 31)], es_sem.at[0], er_sem.at[0])
    all_dh.wait_send()
    all_dh.wait_recv()
    for copy in mine:
        copy.wait()


def dispatch_table(routes, gates, experts):
    names = routes[:, :, None] == experts[None, None, :]
    chosen = jnp.any(names, axis=1)
    gate = jnp.sum(jnp.where(names, gates[:, :, None], 0.0), axis=1)
    tokens = routes.shape[0]
    earlier = jnp.tri(tokens, tokens, -1, dtype=bf16)
    slot = dot(earlier, chosen.astype(bf16)).astype(jnp.int32)
    slot = jnp.where(chosen, slot, -1)
    pick = slot.T[:, None, :] == jnp.arange(CAP, dtype=jnp.int32)[None, :, None]
    slot_gate = jnp.sum(jnp.where(pick, gate.T[:, None, :], 0.0), axis=-1)
    return pick.astype(bf16).reshape(-1, tokens), slot_gate.reshape(-1, 1)


def per_device(
    x_fwd, gate_fwd, route_fwd, x_bwd, gate_bwd, route_bwd, cotangent, norm_gain, w_gate_up, w_down
):
    width = x_fwd.shape[1]
    units = w_down.shape[2]
    slots = 32

    k = jnp.arange(slots, dtype=jnp.int32)
    _, half, z, xl, c = place()
    near = ((z + k % 4) % 4) * 4
    d_b = near + ((xl + k // 16) % 2) * 2 + (c + (k // 8) % 2) % 2
    experts_b = 2 * d_b + (half + (k // 4) % 2) % 2
    j = k % 16
    d_f = ((z + j % 4) % 4) * 4 + ((xl + j // 8) % 2) * 2 + (c + (j // 4) % 2) % 2
    experts_f = 2 * d_f + k // 16

    bwd_hat, bwd_scale = normalize(x_bwd)
    bwd_normed = (bwd_hat * norm_gain).astype(bf16)
    pick_b, slot_gate_b = dispatch_table(route_bwd, gate_bwd, experts_b)
    send_h = dot(pick_b, bwd_normed).astype(bf16)
    send_c = (dot(pick_b, cotangent) * slot_gate_b).astype(bf16)
    fwd_normed = (normalize(x_fwd)[0] * norm_gain).astype(bf16)
    pick_f, slot_gate_f = dispatch_table(route_fwd, gate_fwd, experts_f)
    send_f = dot(pick_f, fwd_normed).astype(bf16)

    rows = slots * CAP
    anywhere = pl.BlockSpec(memory_space=pl.ANY)
    dma = pltpu.SemaphoreType.DMA
    back_f, back_dh, grad_gu, grad_dn = pl.pallas_call(
        kernel,
        out_shape=(
            jax.ShapeDtypeStruct((2, 16, CAP, width), bf16),
            jax.ShapeDtypeStruct((slots, CAP, width), bf16),
            jax.ShapeDtypeStruct((width, width), bf16),
            jax.ShapeDtypeStruct((units, width), bf16),
        ),
        in_specs=[anywhere] * 5,
        out_specs=(anywhere,) * 4,
        scratch_shapes=[
            pltpu.VMEM((2, rows // 2, width), bf16),
            pltpu.VMEM((rows, width), bf16),
            pltpu.VMEM((rows, width), bf16),
            pltpu.VMEM((2, width, width), bf16),
            pltpu.VMEM((2, units, width), bf16),
            pltpu.VMEM((2, rows // 2, width), bf16),
            pltpu.VMEM((rows, width), bf16),
            pltpu.VMEM((PIECE, units), bf16),
            pltpu.VMEM((rows, units), bf16),
            pltpu.VMEM((rows, width), bf16),
            pltpu.VMEM((TILE, rows), bf16),
            pltpu.VMEM((2, TILE, width), bf16),
            dma((2,)), dma((4,)), dma((2, 2)), dma((2, 2)),
            dma((4,)), dma((4,)), dma((4,)), dma((4,)),
            dma((2,)), dma((2,)), dma((1,)), dma((1,)), dma((2,)),
        ],
        compiler_params=pltpu.CompilerParams(
            collective_id=0, has_side_effects=True, vmem_limit_bytes=60 * 1024 * 1024
        ),
    )(
        send_f.reshape(2, 16, CAP, width),
        send_h.reshape(slots, CAP, width),
        send_c.reshape(slots, CAP, width),
        w_gate_up[0],
        w_down[0],
    )

    contract_slots = (((0,), (0,)), ((), ()))
    scaled = (back_f.reshape(rows, width).astype(f32) * slot_gate_f).astype(bf16)
    y_fwd = lax.dot_general(pick_f, scaled, contract_slots, preferred_element_type=f32).astype(bf16)
    dh_sum = lax.dot_general(
        pick_b, back_dh.reshape(rows, width), contract_slots, preferred_element_type=f32
    )
    scaled_dh = norm_gain * dh_sum
    dx_bwd = (
        bwd_scale * (scaled_dh - bwd_hat * jnp.mean(bwd_hat * scaled_dh, axis=-1, keepdims=True))
    ).astype(bf16)
    return y_fwd, dx_bwd, grad_gu[None, None], grad_dn[None, None]


def solution(mesh):
    rows = P(("pipe", "expert"), None)
    weights = P("pipe", "expert", None, None)
    return jax.shard_map(
        per_device,
        mesh=mesh,
        in_specs=(rows,) * 7 + (P(), weights, weights),
        out_specs=(rows, rows, weights, weights),
        check_vma=False,
    )
```

time: 255 us -> 241 us (0.945)
  the two profiles are of different devices: /device:TPU:1 before, /device:TPU:13 now
where the time goes in v2:
time: 241 us
  Pallas kernels  217 us (90%)
  matrix products  12.7 us (5%)
  local copies, waits for them, and re-layouts  5.34 us (2%)
  other arithmetic  5.26 us (2%)
    pallas_call x1, Pallas kernels, per_device(): pl.pallas_call(kernel, out_shape=(jax.ShapeDtypeStruct((2, 16, CAP, width...  217 us
    dot_general x5, matrix products, dot(): return jnp.dot(a, b, preferred_element_type=f32)  8.58 us
    unnamed x22, local copies, waits for them, and re-layouts  5.18 us

profile of v2, /device:TPU:13, one launch (start us, length us, event | category | flops | bytes accessed | tf_op | source)
XLA Modules:
  0.0 241.0 jit_solution(18398458191654580444)
XLA Ops:
  0.6 0.0 copy-start
  0.6 0.0 copy-start.4
  0.7 0.0 copy-start.5
  0.8 0.8 compare_reduce_fusion
  1.6 0.2 fusion.1
  1.8 0.8 compare_reduce_fusion.1
  2.6 0.2 fusion.2
  2.8 0.1 eq.109
  2.9 0.2 bitcast_compare_fusion
  3.1 0.8 fusion.23
  3.9 0.2 select_reduce_fusion.1
  4.2 0.1 mul.137
  4.2 0.0 copy-done
  4.2 0.0 copy-start.1
  4.2 2.7 %multiply_convert_fusion.1 = bf16[1024,1536]{1,0:T(8,128)(2,1)} fusion(pred[1024,128]{1,0:T(32,128)(4,1)S(1)} %get-tuple-element.12, bf16[128,1536]{1,0:T(8,128)(2,1)S(1)} %copy-done, f32[1024]{0:T(1024)S(1)} %mul.137), kind=kOutput, calls=%fused_computation.1 | convolution fusion | flops 405798912 | bytes 3674112 | tf_op jit(solution)/shard_map/dot_general | solution.py:42
  7.0 0.0 copy-done.4
  7.0 0.2 fusion.6
  7.1 0.0 copy-done.5
  7.1 2.7 %convolution_convert_fusion.1 = bf16[1024,1536]{1,0:T(8,128)(2,1)} fusion(pred[1024,128]{1,0:T(32,128)(4,1)S(1)} %get-tuple-element.13, bf16[128,1536]{1,0:T(8,128)(2,1)S(1)} %copy-done.4, f32[1536]{0:T(1024)S(1)} %copy-done.5, f32[128]{0:T(128)S(1)} %add_rsqrt_fusion.1), kind=kOutput, calls=%fused_computation.3 | convolution fusion | flops 405012480 | bytes 3676672 | tf_op jit(solution)/shard_map/dot_general | solution.py:42
  9.9 0.0 copy-done.1
  9.9 0.2 fusion.14
  10.0 2.7 %convolution_convert_fusion = bf16[1024,1536]{1,0:T(8,128)(2,1)} fusion(pred[1024,128]{1,0:T(32,128)(4,1)S(1)} %get-tuple-element.12, bf16[128,1536]{1,0:T(8,128)(2,1)S(1)} %copy-done.1, f32[128]{0:T(128)S(1)} %add_rsqrt_fusion, f32[1536]{0:T(1024)S(1)} %copy-done.5), kind=kOutput, calls=%fused_computation.2 | convolution fusion | flops 405012480 | bytes 3676672 | tf_op jit(solution)/shard_map/dot_general | solution.py:42
  12.8 216.9 %shard_map.129 = (bf16[2,16,32,1536]{3,2,1,0:T(8,128)(2,1)}, bf16[32,32,1536]{2,1,0:T(8,128)(2,1)}, bf16[1536,1536]{1,0:T(8,128)(2,1)}, bf16[768,1536]{1,0:T(8,128)(2,1)}) custom-call(bf16[2,16,32,1536]{3,2,1,0:T(8,128)(2,1)} %bitcast.35, bf16[32,32,1536]{2,1,0:T(8,128)(2,1)} %bitcast.36, bf16[32,32,1536]{2,1,0:T(8,128)(2,1)} %bitcast.34, ...), custom_call_target="tpu_custom_call" | custom-call | tf_op jit(solution)/shard_map/pallas_call | solution.py:298
  229.6 0.0 copy-start.6
  229.6 0.0 copy-start.7
  229.6 0.0 copy-start.2
  229.7 2.8 %fusion.10 = (f32[128]{0:T(128)S(1)}, f32[128,1536]{1,0:T(8,128)S(1)}) fusion(bf16[128,1536]{1,0:T(8,128)(2,1)S(1)} %copy-done.1, f32[128]{0:T(128)S(1)} %add_rsqrt_fusion, bf16[32,32,1536]{2,1,0:T(8,128)(2,1)} %get-tuple-element.9, s32[32,128]{1,0:T(8,128)S(1)} %fusion.1, f32[1536]{0:T(1024)S(1)} %copy-done.5), kind=kOutput, calls=%fused_computation.22 | convolution fusion | flops 403767168 | bytes 4348928 | tf_op jit(solution)/shard_map/dot_general | solution.py:339
  232.4 1.0 fusion.13
  233.5 0.0 copy-done.6
  233.5 0.0 copy-done.7
  233.5 0.1 fusion.22
  233.6 0.2 select_reduce_fusion
  233.8 0.0 slice-start
  233.8 0.0 copy-done.2
  233.8 0.0 slice-start.1
  233.9 0.6 multiply_convert_fusion
  234.4 0.1 iota_compare_fusion.2
  234.5 1.4 convolution_convert_fusion.2
  235.9 0.1 slice-done
  236.0 0.3 slice-done.1
  236.3 0.0 copy-start.3
  236.3 2.4 copy.27
  238.7 1.0 copy-done.3
  239.6 1.4 copy.28
  (7 shorter events, 0.1 us)
Async XLA Ops:
  0.6 3.6 %copy-start = (bf16[128,1536]{1,0:T(8,128)(2,1)S(1)}, bf16[128,1536]{1,0:T(8,128)(2,1)}, u32[]{:S(2)}) copy-start(bf16[128,1536]{1,0:T(8,128)(2,1)} %param.16) | copy-start | bytes 1179652
  0.6 6.3 %copy-start.4 = (bf16[128,1536]{1,0:T(8,128)(2,1)S(1)}, bf16[128,1536]{1,0:T(8,128)(2,1)}, u32[]{:S(2)}) copy-start(bf16[128,1536]{1,0:T(8,128)(2,1)} %param.10) | copy-start | bytes 1179652
  0.7 6.5 %copy-start.5 = (f32[1536]{0:T(1024)S(1)}, f32[1536]{0:T(1024)}, u32[]{:S(2)}) copy-start(f32[1536]{0:T(1024)} %param.17) | copy-start | bytes 18436
  4.2 5.6 %copy-start.1 = (bf16[128,1536]{1,0:T(8,128)(2,1)S(1)}, bf16[128,1536]{1,0:T(8,128)(2,1)}, u32[]{:S(2)}) copy-start(bf16[128,1536]{1,0:T(8,128)(2,1)} %param.13) | copy-start | bytes 1179652
  229.6 3.9 %copy-start.6 = (s32[128,6]{0,1:T(8,128)S(1)}, s32[128,6]{0,1:T(8,128)}, u32[]{:S(2)}) copy-start(s32[128,6]{0,1:T(8,128)} %param.12) | copy-start | bytes 9220
  229.6 3.9 %copy-start.7 = (f32[128,6]{0,1:T(8,128)S(1)}, f32[128,6]{0,1:T(8,128)}, u32[]{:S(2)}) copy-start(f32[128,6]{0,1:T(8,128)} %param.11) | copy-start | bytes 9220
  229.6 4.2 %copy-start.2 = (bf16[2,16,32,1536]{3,2,1,0:T(8,128)(2,1)S(1)}, bf16[2,16,32,1536]{3,2,1,0:T(8,128)(2,1)}, u32[]{:S(2)}) copy-start(bf16[2,16,32,1536]{3,2,1,0:T(8,128)(2,1)} %get-tuple-element.8) | copy-start | bytes 9437188
  233.8 2.2 slice-start
  233.8 2.4 %slice-start.1 = ((s8[4718592]{0:T(1024)(128)(4,1)}), s8[524288]{0:T(1024)(128)(4,1)S(1)}, s32[]{:S(2)}) async-start(s8[4718592]{0:T(1024)(128)(4,1)} %bitcast.38), calls=%async_computation.1 | async-start | bytes 1048576
  236.3 3.4 %copy-start.3 = (bf16[768,1536]{1,0:T(8,128)(2,1)S(1)}, bf16[768,1536]{1,0:T(8,128)(2,1)}, u32[]{:S(2)}) copy-start(bf16[768,1536]{1,0:T(8,128)(2,1)} %get-tuple-element.11) | copy-start | bytes 7077892

commit v3 on v1

v3 whole, which is shorter than its diff:
```python
import jax
import jax.numpy as jnp
from jax import lax
from jax.experimental import pallas as pl
from jax.experimental.pallas import tpu as pltpu
from jax.sharding import PartitionSpec as P

norm_eps = 1e-06
bf16 = jnp.bfloat16
f32 = jnp.float32
MESH = pl.DeviceIdType.MESH
CAP = 32
TILE = 256
WIDE = 512
PIECE = 8 * CAP
HALF = 16 * CAP
NT = (((1,), (1,)), ((), ()))


def place():
    p, d = lax.axis_index("pipe"), lax.axis_index("expert")
    return p, p // 4, d // 4, (d // 2) % 2, d % 2


def peer(sign, kz, kx, kc):
    p, _, z, xl, c = place()
    return p, ((z + sign * kz + 4) % 4) * 4 + ((xl + kx) % 2) * 2 + (c + kc) % 2


def mirror():
    p, _, z, xl, c = place()
    return 7 - p, z * 4 + (1 - xl) * 2 + c


def dot(a, b):
    return jnp.dot(a, b, preferred_element_type=f32)


def dot_nt(a, b):
    return lax.dot_general(a, b, NT, preferred_element_type=f32)


def loop(count, body):
    def step(i, _):
        body(i)
        return 0

    lax.fori_loop(0, count, step, 0)


def kernel(
    x_f, x_b, cot, gain, tab_f, tab_o, tab_m, w_gu, w_dn,
    y_out, dx_out, grad_gu, grad_dn,
    mx, mc, mtab, hf, hb, pick_f, pick_b, sent_f, sent_h, sent_c, got_f, got_h, got_c, gu, dn,
    out_f, out_dh, back_f, back_dh, hid_f, hid, dboth, lhs_t, gout, mine, theirs,
    w_sem, own_sem, ms_sem, mr_sem, fs_sem, fr_sem, hs_sem, hr_sem, cs_sem, cr_sem,
    ds_sem, dr_sem, es_sem, er_sem, ps_sem, pr_sem, g_sem,
):
    width = got_h.shape[1]
    units = dn.shape[1]
    p, half, z, xl, c = place()
    here = (p, z * 4 + xl * 2 + c)
    there = mirror()

    def remote(src, dst, ssem, rsem, to):
        return pltpu.make_async_remote_copy(
            src_ref=src, dst_ref=dst, send_sem=ssem, recv_sem=rsem, device_id=to, device_id_type=MESH
        )

    def landed(dst, ssem, rsem):
        return remote(dst, dst, ssem, rsem, here)

    barrier = pltpu.get_barrier_semaphore()
    pl.semaphore_signal(barrier, inc=1, device_id=there, device_id_type=MESH)

    def greet(k, _):
        to = peer(1, k % 4, k // 8, (k // 4) % 2)
        pl.semaphore_signal(barrier, inc=1, device_id=to, device_id_type=MESH)
        return 0

    lax.fori_loop(1, 16, greet, 0)

    weights = [
        pltpu.make_async_copy(w_gu, gu, w_sem.at[0]),
        pltpu.make_async_copy(w_dn, dn, w_sem.at[1]),
    ]
    for copy in weights:
        copy.start()

    def normalize(src, dst):
        def some(i):
            rows = pl.ds(pl.multiple_of(i * 32, 32), 32)
            v = src[rows, :].astype(f32)
            scale = lax.rsqrt(jnp.mean(v * v, axis=-1, keepdims=True) + norm_eps)
            dst[rows, :] = (v * scale * gain[...]).astype(bf16)

        loop(src.shape[0] // 32, some)

    def picks(table, first, dst, at):
        slots = table[0, first : first + 8, :]
        want = lax.broadcasted_iota(jnp.int32, (8, CAP, 128), 1).astype(f32)
        hit = jnp.where(slots[:, None, :] == want, 1.0, 0.0).reshape(PIECE, 128)
        dst[pl.ds(at, PIECE), :] = hit.astype(bf16)

    def slot_gates(table, first, pick, at):
        gates = table[1, first : first + 8, :]
        each = jnp.broadcast_to(gates[:, None, :], (8, CAP, 128)).reshape(PIECE, 128)
        return jnp.sum(pick[pl.ds(at, PIECE), :].astype(f32) * each, axis=1, keepdims=True)

    def spread(pick, at, src, dst, scale=None):
        def some(t):
            cols = pl.ds(pl.multiple_of(t * WIDE, WIDE), WIDE)
            rows = dot(pick[pl.ds(at, PIECE), :], src[:, cols])
            dst[:, cols] = (rows if scale is None else rows * scale).astype(bf16)

        loop(width // WIDE, some)

    def start_group(a, one):
        lax.fori_loop(1 if a == 0 else 0, 8, one, 0)

    def send_fwd(a):
        def go(j, _):
            to = peer(1, j % 4, a, j // 4)
            rows = pl.ds((a * 8 + j) * CAP, CAP)
            for e in range(2):
                remote(
                    sent_f.at[e, rows], got_f.at[e, rows], fs_sem.at[a, e], fr_sem.at[a, e], to
                ).start()
            return 0

        start_group(a, go)

    def send_bwd(r, a):
        def go(j, _):
            to = peer(1, j % 4, a, j // 4)
            rows = pl.ds(r * HALF + (a * 8 + j) * CAP, CAP)
            remote(sent_h.at[rows], got_h.at[rows], hs_sem.at[r, a], hr_sem.at[r, a], to).start()
            remote(sent_c.at[rows], got_c.at[rows], cs_sem.at[r, a], cr_sem.at[r, a], to).start()
            return 0

        start_group(a, go)

    def return_fwd(a, e):
        def go(j, _):
            to = peer(-1, j % 4, a, j // 4)
            rows = pl.ds((a * 8 + j) * CAP, CAP)
            remote(out_f.at[e, rows], back_f.at[e, rows], ds_sem.at[e], dr_sem.at[e], to).start()
            return 0

        start_group(a, go)

    def return_bwd(r, a):
        def go(j, _):
            to = peer(-1, j % 4, a, j // 4)
            rows = pl.ds(r * HALF + (a * 8 + j) * CAP, CAP)
            remote(out_dh.at[rows], back_dh.at[rows], es_sem.at[r], er_sem.at[r], to).start()
            return 0

        start_group(a, go)

    def span(base, a):
        skip = CAP if a == 0 else 0
        return pl.ds(base + a * PIECE + skip, PIECE - skip)

    def forward_piece(a, e):
        rows = pl.ds(a * PIECE, PIECE)

        def first(t):
            at = pl.multiple_of(t * TILE, TILE)
            x = got_f[e, rows, :]
            gate = dot(x, gu[e, :, pl.ds(at, TILE)])
            up = dot(x, gu[e, :, pl.ds(units + at, TILE)])
            hid_f[:, pl.ds(at, TILE)] = (gate * jax.nn.sigmoid(gate) * up).astype(bf16)

        loop(units // TILE, first)

        def second(t):
            cols = pl.ds(pl.multiple_of(t * TILE, TILE), TILE)
            out_f[e, rows, cols] = dot(hid_f[...], dn[e, :, cols]).astype(bf16)

        loop(width // TILE, second)

    def backward_chain(r, a):
        rows = pl.ds(r * HALF + a * PIECE, PIECE)

        def first(t):
            at = pl.multiple_of(t * TILE, TILE)
            cols = pl.ds(at, TILE)
            more = pl.ds(units + at, TILE)
            x = got_h[rows, :]
            gate = dot(x, gu[half, :, cols])
            up = dot(x, gu[half, :, more])
            back = dot_nt(got_c[rows, :], dn[half, cols, :])
            squash = jax.nn.sigmoid(gate)
            active = gate * squash
            hid[rows, cols] = (active * up).astype(bf16)
            dboth[rows, cols] = (back * up * squash * (1.0 + gate * (1.0 - squash))).astype(bf16)
            dboth[rows, more] = (back * active).astype(bf16)

        loop(units // TILE, first)

        def second(t):
            cols = pl.ds(pl.multiple_of(t * TILE, TILE), TILE)
            out_dh[rows, cols] = dot_nt(dboth[rows, :], gu[half, cols, :]).astype(bf16)

        loop(width // TILE, second)

    def strips(lhs, rhs, count, dst, buf):
        def strip(m):
            at = pl.multiple_of(m * TILE, TILE)
            lhs_t[...] = lhs[:, pl.ds(at, TILE)].T

            def cols_of(t):
                cols = pl.ds(pl.multiple_of(t * TILE, TILE), TILE)
                gout[buf, :, cols] = dot(lhs_t[...], rhs[:, cols]).astype(bf16)

            loop(width // TILE, cols_of)
            copy = pltpu.make_async_copy(gout.at[buf], dst.at[pl.ds(at, TILE)], g_sem.at[buf])
            copy.start()
            copy.wait()

        loop(count, strip)

    normalize(x_f, hf)
    for e in range(2):
        for a in range(2):
            at = e * HALF + a * PIECE
            picks(tab_f, e * 16 + a * 8, pick_f, at)
            spread(pick_f, at, hf, sent_f.at[e, pl.ds(a * PIECE, PIECE)])
    pl.semaphore_wait(barrier, 16)
    over = [
        remote(x_b, mx, ms_sem.at[0], mr_sem.at[0], there),
        remote(cot, mc, ms_sem.at[1], mr_sem.at[1], there),
        remote(tab_m, mtab, ms_sem.at[2], mr_sem.at[2], there),
    ]
    for copy in over:
        copy.start()
    send_fwd(0)
    send_fwd(1)
    own = [
        pltpu.make_async_copy(
            sent_f.at[e, pl.ds(0, CAP)], got_f.at[e, pl.ds(0, CAP)], own_sem.at[e]
        )
        for e in range(2)
    ]

    def dispatch(r, table, x_rows, c_rows):
        for a in range(2):
            at = r * HALF + a * PIECE
            picks(table, a * 8, pick_b, at)
            spread(pick_b, at, x_rows, sent_h.at[pl.ds(at, PIECE)])
            gates = slot_gates(table, a * 8, pick_b, at)
            spread(pick_b, at, c_rows, sent_c.at[pl.ds(at, PIECE)], gates)

    normalize(x_b, hb)
    dispatch(0, tab_o, hb, cot)
    for copy in over:
        copy.wait_recv()
    normalize(mx, hf)
    dispatch(1, mtab, hf, mc)
    send_bwd(1, 0)
    send_bwd(1, 1)
    for r in range(2):
        rows = pl.ds(r * HALF, CAP)
        own.append(pltpu.make_async_copy(sent_h.at[rows], got_h.at[rows], own_sem.at[2 + r]))
        own.append(pltpu.make_async_copy(sent_c.at[rows], got_c.at[rows], own_sem.at[4 + r]))
    for copy in own:
        copy.start()
    for copy in weights:
        copy.wait()
    for copy in own:
        copy.wait()

    for a in range(2):
        for e in range(2):
            landed(got_f.at[e, span(0, a)], fs_sem.at[a, e], fr_sem.at[a, e]).wait_recv()
        send_bwd(0, a)
        for e in range(2):
            forward_piece(a, e)
            return_fwd(a, e)
    for r in (1, 0):
        for a in range(2):
            where = span(r * HALF, a)
            landed(got_h.at[where], hs_sem.at[r, a], hr_sem.at[r, a]).wait_recv()
            landed(got_c.at[where], cs_sem.at[r, a], cr_sem.at[r, a]).wait_recv()
            backward_chain(r, a)
            return_bwd(r, a)

    home = [
        pltpu.make_async_copy(
            out_f.at[e, pl.ds(0, CAP)], back_f.at[e, pl.ds(0, CAP)], own_sem.at[e]
        )
        for e in range(2)
    ]
    for r in range(2):
        rows = pl.ds(r * HALF, CAP)
        home.append(pltpu.make_async_copy(out_dh.at[rows], back_dh.at[rows], own_sem.at[2 + r]))
    for copy in home:
        copy.start()
    for copy in home:
        copy.wait()

    strips(hid, got_c, units // TILE, grad_dn, 1)

    def returned(r):
        return landed(
            back_dh.at[pl.ds(r * HALF + CAP, HALF - CAP)], es_sem.at[r], er_sem.at[r]
        )

    def gathered(r, cols):
        total = None
        for a in range(2):
            rows = pl.ds(r * HALF + a * PIECE, PIECE)
            part = dot(pick_b[rows, :].T, back_dh[rows, cols])
            total = part if total is None else total + part
        return total

    returned(1).wait_recv()

    def sum_mirror(t):
        cols = pl.ds(pl.multiple_of(t * WIDE, WIDE), WIDE)
        mine[:, cols] = gathered(1, cols).astype(bf16)

    loop(width // WIDE, sum_mirror)
    back_home = remote(mine, theirs, ps_sem.at[0], pr_sem.at[0], there)
    back_home.start()

    strips(got_h, dboth, width // TILE, grad_gu, 0)

    for e in range(2):
        landed(back_f.at[e, pl.ds(CAP, HALF - CAP)], ds_sem.at[e], dr_sem.at[e]).wait_recv()
    for e in range(2):
        for a in range(2):
            rows = pl.ds(a * PIECE, PIECE)
            gates = slot_gates(tab_f, e * 16 + a * 8, pick_f, e * HALF + a * PIECE)
            out_f_rows = back_f[e, rows, :].astype(f32) * gates
            back_f[e, rows, :] = out_f_rows.astype(bf16)

    def sum_fwd(t):
        cols = pl.ds(pl.multiple_of(t * WIDE, WIDE), WIDE)
        total = None
        for e in range(2):
            for a in range(2):
                pick = pick_f[pl.ds(e * HALF + a * PIECE, PIECE), :].T
                part = dot(pick, back_f[e, pl.ds(a * PIECE, PIECE), cols])
                total = part if total is None else total + part
        y_out[:, cols] = total.astype(bf16)

    loop(width // WIDE, sum_fwd)

    returned(0).wait_recv()
    back_home.wait_recv()

    def finish(dx_sum):
        def own_cols(t):
            cols = pl.ds(pl.multiple_of(t * WIDE, WIDE), WIDE)
            dx_sum[:, cols] = gathered(0, cols) + theirs[:, cols].astype(f32)

        loop(width // WIDE, own_cols)

        def some(i):
            rows = pl.ds(pl.multiple_of(i * 32, 32), 32)
            v = x_b[rows, :].astype(f32)
            scale = lax.rsqrt(jnp.mean(v * v, axis=-1, keepdims=True) + norm_eps)
            hat = v * scale
            q = gain[...] * dx_sum[rows, :]
            dx = scale * (q - hat * jnp.mean(hat * q, axis=-1, keepdims=True))
            dx_out[rows, :] = dx.astype(bf16)

        loop(x_b.shape[0] // 32, some)

    pl.run_scoped(finish, pltpu.VMEM((128, width), f32))

    for copy in over:
        copy.wait_send()
    back_home.wait_send()
    for a in range(2):
        for e in range(2):
            landed(got_f.at[e, span(0, a)], fs_sem.at[a, e], fr_sem.at[a, e]).wait_send()
        for r in range(2):
            where = span(r * HALF, a)
            landed(got_h.at[where], hs_sem.at[r, a], hr_sem.at[r, a]).wait_send()
            landed(got_c.at[where], cs_sem.at[r, a], cr_sem.at[r, a]).wait_send()
    for e in range(2):
        landed(back_f.at[e, pl.ds(CAP, HALF - CAP)], ds_sem.at[e], dr_sem.at[e]).wait_send()
    for r in range(2):
        returned(r).wait_send()


def slot_table(routes, gates, experts):
    names = routes[:, :, None] == experts[None, None, :]
    chosen = jnp.any(names, axis=1)
    gate = jnp.sum(jnp.where(names, gates[:, :, None], 0.0), axis=1)
    tokens = routes.shape[0]
    earlier = jnp.tri(tokens, tokens, -1, dtype=bf16)
    slot = jnp.where(chosen, dot(earlier, chosen.astype(bf16)), -1.0)
    return jnp.stack([slot.T, gate.T])


def per_device(
    x_fwd, gate_fwd, route_fwd, x_bwd, gate_bwd, route_bwd, cotangent, norm_gain, w_gate_up, w_down
):
    tokens, width = x_fwd.shape
    units = w_down.shape[2]

    _, half, z, xl, c = place()
    k = jnp.arange(32, dtype=jnp.int32)
    s, second = k % 16, k // 16

    def device_of(flip):
        return ((z + s % 4) % 4) * 4 + ((xl + flip + s // 8) % 2) * 2 + (c + (s // 4) % 2) % 2

    table_f = slot_table(route_fwd, gate_fwd, 2 * device_of(0) + second)
    table_b = slot_table(route_bwd, gate_bwd, 2 * device_of(second) + (half + second) % 2)

    rows = 32 * CAP
    anywhere = pl.BlockSpec(memory_space=pl.ANY)
    vmem = pl.BlockSpec(memory_space=pltpu.VMEM)
    dma = pltpu.SemaphoreType.DMA

    def hold(*shape, dtype=bf16):
        return pltpu.VMEM(shape, dtype)

    y_fwd, dx_bwd, grad_gu, grad_dn = pl.pallas_call(
        kernel,
        out_shape=(
            jax.ShapeDtypeStruct((tokens, width), bf16),
            jax.ShapeDtypeStruct((tokens, width), bf16),
            jax.ShapeDtypeStruct((width, width), bf16),
            jax.ShapeDtypeStruct((units, width), bf16),
        ),
        in_specs=[vmem] * 7 + [anywhere] * 2,
        out_specs=(vmem, vmem, anywhere, anywhere),
        scratch_shapes=[
            hold(tokens, width),
            hold(tokens, width),
            hold(2, 16, tokens, dtype=f32),
            hold(tokens, width),
            hold(tokens, width),
            hold(rows, tokens),
            hold(rows, tokens),
            hold(2, HALF, width),
            hold(rows, width),
            hold(rows, width),
            hold(2, HALF, width),
            hold(rows, width),
            hold(rows, width),
            hold(2, width, width),
            hold(2, units, width),
            hold(2, HALF, width),
            hold(rows, width),
            hold(2, HALF, width),
            hold(rows, width),
            hold(PIECE, units),
            hold(rows, units),
            hold(rows, width),
            hold(TILE, rows),
            hold(2, TILE, width),
            hold(tokens, width),
            hold(tokens, width),
            dma((2,)), dma((6,)), dma((3,)), dma((3,)), dma((2, 2)), dma((2, 2)),
            dma((2, 2)), dma((2, 2)), dma((2, 2)), dma((2, 2)),
            dma((2,)), dma((2,)), dma((2,)), dma((2,)), dma((1,)), dma((1,)), dma((2,)),
        ],
        compiler_params=pltpu.CompilerParams(
            collective_id=0, has_side_effects=True, vmem_limit_bytes=67043328
        ),
    )(
        x_fwd,
        x_bwd,
        cotangent,
        norm_gain.reshape(1, width),
        table_f,
        table_b[:, :16],
        table_b[:, 16:],
        w_gate_up[0],
        w_down[0],
    )
    return y_fwd, dx_bwd, grad_gu[None, None], grad_dn[None, None]


def solution(mesh):
    rows = P(("pipe", "expert"), None)
    weights = P("pipe", "expert", None, None)
    return jax.shard_map(
        per_device,
        mesh=mesh,
        in_specs=(rows,) * 7 + (P(), weights, weights),
        out_specs=(rows, rows, weights, weights),
        check_vma=False,
    )
```

time: 255 us -> 208 us (0.82); the launches traced: 250 us -> 207 us
  Pallas kernels: 0 us -> 190 us
  waiting for transfers between devices: 126 us -> 0 us
  matrix products: 68.6 us -> 0.42 us
  starting transfers between devices: 33 us -> 0 us
  other arithmetic: 8.25 us -> 4.4 us
    pallas_call x0 -> x1, Pallas kernels: none -> 190 us  [per_device(): pl.pallas_call(kernel, out_shape=(jax.ShapeDtypeStruct((tokens, width), b...]
    all_to_all x5 -> x0, waiting for transfers between devices: 126 us -> none  [the longest x3 85.3 us: exchange_pair(): lax.all_to_all(value, ('pipe', 'expert'), split_axis=0, concat_axis=0, ax...]
    dot_general x14 -> x2, matrix products: 68.6 us -> 0.42 us  [dot(): return jnp.dot(a, b, preferred_element_type=f32)]
    all_to_all x5 -> x0, starting transfers between devices: 33 us -> none  [the longest x3 20 us: exchange_pair(): lax.all_to_all(value, ('pipe', 'expert'), split_axis=0, concat_axis=0, ax...]
    unnamed x50 -> x6, local copies, waits for them, and re-layouts: 6.5 us -> 9.92 us
    eq x5 -> x0, local copies, waits for them, and re-layouts: 2.69 us -> none  [dispatch_table(): slot.T[:, None, :] == jnp.arange(capacity, dtype=jnp.int32)[None, :, None]]
    eq x4 -> x0, other arithmetic: 2.62 us -> none  [dispatch_table(): slot.T[:, None, :] == jnp.arange(capacity, dtype=jnp.int32)[None, :, None]]
  transfers between devices with their start and end apart: 5 -> 0, of which waited for: 5 -> 0; matrix products, arithmetic and copies ran while one was open for 29% -> 0% of each run, Pallas kernels for 0% -> 0%
where the time goes in v3:
time: 208 us; the launch traced here: 207 us
  Pallas kernels  190 us (91%)
  local copies, waits for them, and re-layouts  11.2 us (5%)
  other arithmetic  4.4 us (2%)
    pallas_call x1, Pallas kernels, per_device(): pl.pallas_call(kernel, out_shape=(jax.ShapeDtypeStruct((tokens, width), b...  190 us
    unnamed x6, local copies, waits for them, and re-layouts  9.92 us

profile of v3, /device:TPU:1, one launch (start us, length us, event | category | flops | bytes accessed | tf_op | source)
XLA Modules:
  0.0 206.7 jit_solution(1477545027366031515)
XLA Ops:
  0.7 0.8 compare_reduce_fusion.1
  1.5 0.8 compare_reduce_fusion
  2.3 1.3 reshape.156.gain
  3.6 0.2 fusion
  3.8 0.2 fusion.1
  4.0 0.8 fusion.3
  4.8 0.6 pad_maximum_fusion.1
  5.4 0.8 fusion.2
  6.2 0.6 pad_maximum_fusion.tab_f
  6.8 190.0 %shard_map.129 = (bf16[128,1536]{1,0:T(8,128)(2,1)}, bf16[128,1536]{1,0:T(8,128)(2,1)}, bf16[1536,1536]{1,0:T(8,128)(2,1)}, bf16[768,1536]{1,0:T(8,128)(2,1)}) custom-call(bf16[128,1536]{1,0:T(8,128)(2,1)} %x_f.1, bf16[128,1536]{1,0:T(8,128)(2,1)} %x_b.1, bf16[128,1536]{1,0:T(8,128)(2,1)} %cot.1, f32[1,1536]{1,0:T(1,128)} %reshape.156.gain, ...), custom_call_target="tpu_custom_call" | custom-call | tf_op jit(solution)/shard_map/pallas_call | solution.py:424
  196.8 1.8 copy.22
  198.6 1.8 copy.23
  200.3 0.0 copy-start
  200.3 5.0 %copy.24 = bf16[1,1,1536,1536]{3,2,1,0:T(8,128)(2,1)} copy(bf16[1,1,1536,1536]{3,2,1,0:T(8,128)(2,1)} %bitcast.22) | data formatting | bytes 9437184
  205.3 0.0 copy-done
  205.3 1.4 copy.25
  (2 shorter events, 0.0 us)
Async XLA Ops:
  200.3 5.0 %copy-start = (bf16[768,1536]{1,0:T(8,128)(2,1)S(1)}, bf16[768,1536]{1,0:T(8,128)(2,1)}, u32[]{:S(2)}) copy-start(bf16[768,1536]{1,0:T(8,128)(2,1)} %get-tuple-element.11) | copy-start | bytes 7077892

commit v4 on v3

v4 whole, which is shorter than its diff:
```python
import jax
import jax.numpy as jnp
from jax import lax
from jax.experimental import pallas as pl
from jax.experimental.pallas import tpu as pltpu
from jax.sharding import PartitionSpec as P

norm_eps = 1e-06
bf16 = jnp.bfloat16
f32 = jnp.float32
MESH = pl.DeviceIdType.MESH
CAP = 32
TILE = 256
WIDE = 512
PIECE = 8 * CAP
NT = (((1,), (1,)), ((), ()))


def place():
    p, d = lax.axis_index("pipe"), lax.axis_index("expert")
    return p, p // 4, d // 4, (d // 2) % 2, d % 2


def peer(kz, kx, kc, kh):
    p, _, z, xl, c = place()
    return p + kh * (7 - 2 * p), ((z + kz + 4) % 4) * 4 + ((xl + kx) % 2) * 2 + (c + kc) % 2


def dot(a, b):
    return jnp.dot(a, b, preferred_element_type=f32)


def dot_nt(a, b):
    return lax.dot_general(a, b, NT, preferred_element_type=f32)


def loop(count, body):
    def step(i, _):
        body(i)
        return 0

    lax.fori_loop(0, count, step, 0)


def kernel(
    x_f, x_b, cot, gain, tab_f, tab_b, w_gu, w_dn,
    y_out, dx_out, grad_gu, grad_dn,
    zx, ztab, mx, mc, mtab, normed, pick_f, pick_b, sent_f, sent_h, sent_c, got_f, got_h, got_c,
    gu, dn, out_f, out_dh, back_f, back_dh, hid_f, hid, dboth, lhs_t, gout, sums_f, sums_b, total,
    w_sem, own_sem, zs_sem, zr_sem, ms_sem, mr_sem, fs_sem, fr_sem, hs_sem, hr_sem, cs_sem, cr_sem,
    ds_sem, dr_sem, es_sem, er_sem, qs_sem, qr_sem, ps_sem, pr_sem, g_sem,
):
    width = got_h.shape[1]
    units = dn.shape[1]
    half = place()[1]
    here = peer(0, 0, 0, 0)

    def remote(src, dst, ssem, rsem, to):
        return pltpu.make_async_remote_copy(
            src_ref=src, dst_ref=dst, send_sem=ssem, recv_sem=rsem, device_id=to, device_id_type=MESH
        )

    def landed(dst, ssem, rsem):
        return remote(dst, dst, ssem, rsem, here)

    barrier = pltpu.get_barrier_semaphore()
    others = [(kz, 0, kc, 0) for kc in range(2) for kz in range(4)][1:]
    others += [(0, 1, 0, 0), (0, 1, 1, 0), (0, 0, 0, 1), (0, 1, 0, 1)]
    for other in others:
        pl.semaphore_signal(barrier, inc=1, device_id=peer(*other), device_id_type=MESH)

    weights = [
        pltpu.make_async_copy(w_gu, gu, w_sem.at[0]),
        pltpu.make_async_copy(w_dn, dn, w_sem.at[1]),
    ]
    for copy in weights:
        copy.start()

    def normalize(src, dst):
        def some(i):
            rows = pl.ds(pl.multiple_of(i * 32, 32), 32)
            v = src[rows, :].astype(f32)
            scale = lax.rsqrt(jnp.mean(v * v, axis=-1, keepdims=True) + norm_eps)
            dst[rows, :] = (v * scale * gain[...]).astype(bf16)

        loop(src.shape[0] // 32, some)

    def picks(slots, dst):
        want = lax.broadcasted_iota(jnp.int32, (8, CAP, 128), 1).astype(f32)
        hit = jnp.where(slots[:, None, :] == want, 1.0, 0.0).reshape(PIECE, 128)
        dst[...] = hit.astype(bf16)

    def slot_gates(gates, pick):
        each = jnp.broadcast_to(gates[:, None, :], (8, CAP, 128)).reshape(PIECE, 128)
        return jnp.sum(pick[...].astype(f32) * each, axis=1, keepdims=True)

    def wide(body):
        loop(width // WIDE, lambda t: body(pl.ds(pl.multiple_of(t * WIDE, WIDE), WIDE)))

    def over_z(k):
        return [
            remote(x_f, zx.at[k - 1], zs_sem.at[0, k - 1], zr_sem.at[0, k - 1], peer(k, 0, 0, 0)),
            remote(
                tab_f.at[k], ztab.at[k - 1], zs_sem.at[1, k - 1], zr_sem.at[1, k - 1],
                peer(k, 0, 0, 0),
            ),
        ]

    def over_x(r):
        to = peer(0, r % 2, 0, r // 2)
        i = r - 1
        return [
            remote(x_b, mx.at[i], ms_sem.at[0, i], mr_sem.at[0, i], to),
            remote(cot, mc.at[i], ms_sem.at[1, i], mr_sem.at[1, i], to),
            remote(tab_b.at[r], mtab.at[i], ms_sem.at[2, i], mr_sem.at[2, i], to),
        ]

    raw_z = [over_z(k) for k in (1, 2, 3)]
    raw_x = [over_x(r) for r in (1, 2, 3)]

    def send_fwd(e, slot):
        return remote(
            sent_f.at[e * 4 + slot], got_f.at[e, slot], fs_sem.at[e, slot - 1], fr_sem.at[e, slot - 1],
            peer(0, slot // 2, slot % 2, 0),
        )

    def return_fwd(e, slot):
        return remote(
            out_f.at[e, slot], back_f.at[e * 4 + slot], ds_sem.at[e, slot - 1],
            dr_sem.at[e, slot - 1], peer(0, slot // 2, slot % 2, 0),
        )

    def send_bwd(r):
        def go(j, _):
            to = peer(j % 4, 0, j // 4, 0)
            rows = pl.ds(r * PIECE + j * CAP, CAP)
            remote(sent_h.at[rows], got_h.at[rows], hs_sem.at[r], hr_sem.at[r], to).start()
            remote(sent_c.at[rows], got_c.at[rows], cs_sem.at[r], cr_sem.at[r], to).start()
            return 0

        lax.fori_loop(1, 8, go, 0)
        first = pl.ds(r * PIECE, CAP)
        pltpu.make_async_copy(sent_h.at[first], got_h.at[first], own_sem.at[0, r]).start()
        pltpu.make_async_copy(sent_c.at[first], got_c.at[first], own_sem.at[1, r]).start()

    def return_bwd(r):
        def go(j, _):
            to = peer(-(j % 4), 0, j // 4, 0)
            rows = pl.ds(r * PIECE + j * CAP, CAP)
            remote(out_dh.at[rows], back_dh.at[rows], es_sem.at[r], er_sem.at[r], to).start()
            return 0

        lax.fori_loop(1, 8, go, 0)
        first = pl.ds(r * PIECE, CAP)
        pltpu.make_async_copy(out_dh.at[first], back_dh.at[first], own_sem.at[2, r]).start()

    def rest(r):
        return pl.ds(r * PIECE + CAP, PIECE - CAP)

    def all_of(ref, r):
        return ref.at[pl.ds(r * PIECE, CAP)]

    def forward_piece(a, e):
        def first(t):
            at = pl.multiple_of(t * TILE, TILE)
            x = got_f[e, 2 * a : 2 * a + 2].reshape(PIECE, width)
            gate = dot(x, gu[e, :, pl.ds(at, TILE)])
            up = dot(x, gu[e, :, pl.ds(units + at, TILE)])
            hid_f[:, pl.ds(at, TILE)] = (gate * jax.nn.sigmoid(gate) * up).astype(bf16)

        loop(units // TILE, first)

        def second(t):
            cols = pl.ds(pl.multiple_of(t * TILE, TILE), TILE)
            rows = dot(hid_f[...], dn[e, :, cols]).astype(bf16)
            out_f[e, 2 * a : 2 * a + 2, :, :, cols] = rows.reshape(2, 4, CAP, TILE)

        loop(width // TILE, second)

    def backward_chain(r):
        rows = pl.ds(r * PIECE, PIECE)

        def first(t):
            at = pl.multiple_of(t * TILE, TILE)
            cols = pl.ds(at, TILE)
            more = pl.ds(units + at, TILE)
            x = got_h[rows, :]
            gate = dot(x, gu[half, :, cols])
            up = dot(x, gu[half, :, more])
            back = dot_nt(got_c[rows, :], dn[half, cols, :])
            squash = jax.nn.sigmoid(gate)
            active = gate * squash
            hid[rows, cols] = (active * up).astype(bf16)
            dboth[rows, cols] = (back * up * squash * (1.0 + gate * (1.0 - squash))).astype(bf16)
            dboth[rows, more] = (back * active).astype(bf16)

        loop(units // TILE, first)

        def second(t):
            cols = pl.ds(pl.multiple_of(t * TILE, TILE), TILE)
            out_dh[rows, cols] = dot_nt(dboth[rows, :], gu[half, cols, :]).astype(bf16)

        loop(width // TILE, second)

    def strips(lhs, rhs, count, dst, buf):
        def strip(m):
            at = pl.multiple_of(m * TILE, TILE)
            lhs_t[...] = lhs[:, pl.ds(at, TILE)].T

            def cols_of(t):
                cols = pl.ds(pl.multiple_of(t * TILE, TILE), TILE)
                gout[buf, :, cols] = dot(lhs_t[...], rhs[:, cols]).astype(bf16)

            loop(width // TILE, cols_of)
            copy = pltpu.make_async_copy(gout.at[buf], dst.at[pl.ds(at, TILE)], g_sem.at[buf])
            copy.start()
            copy.wait()

        loop(count, strip)

    def dispatch_fwd(b, table):
        picks(table[0], pick_f.at[b])

        def some(cols):
            rows = dot(pick_f[b], normed[:, cols]).astype(bf16)
            sent_f[:, b, :, cols] = rows.reshape(8, CAP, WIDE)

        wide(some)

    def dispatch_bwd(r, table, c_rows):
        picks(table[0], pick_b.at[r])
        gates = slot_gates(table[1], pick_b.at[r])
        rows = pl.ds(r * PIECE, PIECE)

        def some(cols):
            sent_h[rows, cols] = dot(pick_b[r], normed[:, cols]).astype(bf16)
            sent_c[rows, cols] = (dot(pick_b[r], c_rows[:, cols]) * gates).astype(bf16)

        wide(some)

    normalize(x_b, normed)
    pl.semaphore_wait(barrier, len(others))
    for copies in raw_z + [raw_x[0], raw_x[2], raw_x[1]]:
        for copy in copies:
            copy.start()
    dispatch_bwd(0, tab_b.at[0], cot)
    send_bwd(0)

    normalize(x_f, normed)
    dispatch_fwd(0, tab_f.at[0])
    for k in (1, 3, 2):
        for copy in raw_z[k - 1]:
            copy.wait_recv()
        normalize(zx.at[k - 1], normed)
        dispatch_fwd(k, ztab.at[k - 1])
    own_f = [
        pltpu.make_async_copy(sent_f.at[e * 4], got_f.at[e, 0], own_sem.at[3, e]) for e in range(2)
    ]
    for copy in own_f:
        copy.start()
    for slot in (2, 3, 1):
        for e in range(2):
            send_fwd(e, slot).start()
    for r in (1, 3, 2):
        for copy in raw_x[r - 1]:
            copy.wait_recv()
        normalize(mx.at[r - 1], normed)
        dispatch_bwd(r, mtab.at[r - 1], mc.at[r - 1])
        send_bwd(r)
    for copy in weights + own_f:
        copy.wait()

    def forward(a):
        for e in range(2):
            for slot in (2 * a, 2 * a + 1):
                if slot:
                    send_fwd(e, slot).wait_recv()
        for e in range(2):
            forward_piece(a, e)
            for slot in (2 * a, 2 * a + 1):
                if slot:
                    return_fwd(e, slot).start()

    def backward(r):
        landed(got_h.at[rest(r)], hs_sem.at[r], hr_sem.at[r]).wait_recv()
        landed(got_c.at[rest(r)], cs_sem.at[r], cr_sem.at[r]).wait_recv()
        pltpu.make_async_copy(all_of(sent_h, r), all_of(got_h, r), own_sem.at[0, r]).wait()
        pltpu.make_async_copy(all_of(sent_c, r), all_of(got_c, r), own_sem.at[1, r]).wait()
        backward_chain(r)
        return_bwd(r)

    forward(0)
    backward(0)
    backward(1)
    forward(1)
    home = [
        pltpu.make_async_copy(out_f.at[e, 0], back_f.at[e * 4], own_sem.at[3, e]) for e in range(2)
    ]
    for copy in home:
        copy.start()
    backward(3)
    backward(2)
    strips(hid, got_c, units // TILE, grad_dn, 1)

    def returned(r):
        return landed(back_dh.at[rest(r)], es_sem.at[r], er_sem.at[r])

    def gathered_bwd(r, cols):
        return dot(pick_b[r].T, back_dh[pl.ds(r * PIECE, PIECE), cols])

    def home_bwd(r):
        returned(r).wait_recv()
        pltpu.make_async_copy(all_of(out_dh, r), all_of(back_dh, r), own_sem.at[2, r]).wait()

    back_x = []
    for r in (1, 3, 2):
        home_bwd(r)

        def sum_block(cols):
            mx[r - 1, :, cols] = gathered_bwd(r, cols).astype(bf16)

        wide(sum_block)
        copy = remote(
            mx.at[r - 1], sums_b.at[r - 1], ps_sem.at[r - 1], pr_sem.at[r - 1],
            peer(0, r % 2, 0, r // 2),
        )
        copy.start()
        back_x.append(copy)

    for e in range(2):
        for slot in (1, 2, 3):
            return_fwd(e, slot).wait_recv()
    for copy in home:
        copy.wait()

    def gated_rows(b, table):
        gates = slot_gates(table[1], pick_f.at[b])
        rows = back_f[:, b].reshape(PIECE, width).astype(f32) * gates
        lhs = rows.astype(bf16)
        back_f[:, b] = lhs.reshape(8, CAP, width)

    def gathered_fwd(b, cols):
        return dot(pick_f[b].T, back_f[:, b, :, cols].reshape(PIECE, WIDE))

    back_z = []
    for b in (2, 1, 3):
        gated_rows(b, ztab.at[b - 1])

        def sum_rows(cols):
            zx[b - 1, :, cols] = gathered_fwd(b, cols).astype(bf16)

        wide(sum_rows)
        copy = remote(
            zx.at[b - 1], sums_f.at[b - 1], qs_sem.at[b - 1], qr_sem.at[b - 1], peer(-b, 0, 0, 0)
        )
        copy.start()
        back_z.append(copy)
    gated_rows(0, tab_f.at[0])

    strips(got_h, dboth, width // TILE, grad_gu, 0)

    home_bwd(0)

    def own_dh(cols):
        total[:, cols] = gathered_bwd(0, cols)

    wide(own_dh)
    for copy in back_z:
        copy.wait_recv()

    def own_y(cols):
        y = gathered_fwd(0, cols)
        for i in range(3):
            y = y + sums_f[i, :, cols].astype(f32)
        y_out[:, cols] = y.astype(bf16)

    wide(own_y)
    for copy in back_x:
        copy.wait_recv()

    def finish(i):
        rows = pl.ds(pl.multiple_of(i * 32, 32), 32)
        v = x_b[rows, :].astype(f32)
        scale = lax.rsqrt(jnp.mean(v * v, axis=-1, keepdims=True) + norm_eps)
        hat = v * scale
        dh = total[rows, :]
        for n in range(3):
            dh = dh + sums_b[n, rows, :].astype(f32)
        q = gain[...] * dh
        dx = scale * (q - hat * jnp.mean(hat * q, axis=-1, keepdims=True))
        dx_out[rows, :] = dx.astype(bf16)

    loop(x_b.shape[0] // 32, finish)

    for copies in raw_z + raw_x:
        for copy in copies:
            copy.wait_send()
    for copy in back_x + back_z:
        copy.wait_send()
    for e in range(2):
        for slot in (1, 2, 3):
            send_fwd(e, slot).wait_send()
            return_fwd(e, slot).wait_send()
    for r in range(4):
        landed(got_h.at[rest(r)], hs_sem.at[r], hr_sem.at[r]).wait_send()
        landed(got_c.at[rest(r)], cs_sem.at[r], cr_sem.at[r]).wait_send()
        returned(r).wait_send()


def slot_table(routes, gates, experts):
    names = routes[:, :, None] == experts[None, None, :]
    chosen = jnp.any(names, axis=1)
    gate = jnp.sum(jnp.where(names, gates[:, :, None], 0.0), axis=1)
    tokens = routes.shape[0]
    earlier = jnp.tri(tokens, tokens, -1, dtype=bf16)
    slot = jnp.where(chosen, dot(earlier, chosen.astype(bf16)), -1.0)
    return jnp.stack([slot.T.reshape(4, 8, tokens), gate.T.reshape(4, 8, tokens)], axis=1)


def per_device(
    x_fwd, gate_fwd, route_fwd, x_bwd, gate_bwd, route_bwd, cotangent, norm_gain, w_gate_up, w_down
):
    tokens, width = x_fwd.shape
    units = w_down.shape[2]

    _, half, z, xl, c = place()
    k = jnp.arange(32, dtype=jnp.int32)
    agent, s = k // 8, k % 8
    core = (c + s // 4) % 2
    d_f = ((z + agent) % 4) * 4 + ((xl + (s // 2) % 2) % 2) * 2 + (c + s % 2) % 2
    d_b = ((z + s % 4) % 4) * 4 + ((xl + agent % 2) % 2) * 2 + core
    table_f = slot_table(route_fwd, gate_fwd, 2 * d_f + s // 4)
    table_b = slot_table(route_bwd, gate_bwd, 2 * d_b + (half + agent // 2) % 2)

    rows = 32 * CAP
    anywhere = pl.BlockSpec(memory_space=pl.ANY)
    vmem = pl.BlockSpec(memory_space=pltpu.VMEM)
    dma = pltpu.SemaphoreType.DMA

    def hold(*shape, dtype=bf16):
        return pltpu.VMEM(shape, dtype)

    y_fwd, dx_bwd, grad_gu, grad_dn = pl.pallas_call(
        kernel,
        out_shape=(
            jax.ShapeDtypeStruct((tokens, width), bf16),
            jax.ShapeDtypeStruct((tokens, width), bf16),
            jax.ShapeDtypeStruct((width, width), bf16),
            jax.ShapeDtypeStruct((units, width), bf16),
        ),
        in_specs=[vmem] * 6 + [anywhere] * 2,
        out_specs=(vmem, vmem, anywhere, anywhere),
        scratch_shapes=[
            hold(3, tokens, width),
            hold(3, 2, 8, tokens, dtype=f32),
            hold(3, tokens, width),
            hold(3, tokens, width),
            hold(3, 2, 8, tokens, dtype=f32),
            hold(tokens, width),
            hold(4, PIECE, tokens),
            hold(4, PIECE, tokens),
            hold(8, 4, CAP, width),
            hold(rows, width),
            hold(rows, width),
            hold(2, 4, 4, CAP, width),
            hold(rows, width),
            hold(rows, width),
            hold(2, width, width),
            hold(2, units, width),
            hold(2, 4, 4, CAP, width),
            hold(rows, width),
            hold(8, 4, CAP, width),
            hold(rows, width),
            hold(PIECE, units),
            hold(rows, units),
            hold(rows, width),
            hold(TILE, rows),
            hold(2, TILE, width),
            hold(3, tokens, width),
            hold(3, tokens, width),
            hold(tokens, width, dtype=f32),
            dma((2,)), dma((4, 4)), dma((2, 3)), dma((2, 3)), dma((3, 3)), dma((3, 3)),
            dma((2, 3)), dma((2, 3)), dma((4,)), dma((4,)), dma((4,)), dma((4,)),
            dma((2, 3)), dma((2, 3)), dma((4,)), dma((4,)), dma((3,)), dma((3,)),
            dma((3,)), dma((3,)), dma((2,)),
        ],
        compiler_params=pltpu.CompilerParams(
            collective_id=0, has_side_effects=True, vmem_limit_bytes=67043328
        ),
    )(
        x_fwd,
        x_bwd,
        cotangent,
        norm_gain.reshape(1, width),
        table_f,
        table_b,
        w_gate_up[0],
        w_down[0],
    )
    return y_fwd, dx_bwd, grad_gu[None, None], grad_dn[None, None]


def solution(mesh):
    rows = P(("pipe", "expert"), None)
    weights = P("pipe", "expert", None, None)
    return jax.shard_map(
        per_device,
        mesh=mesh,
        in_specs=(rows,) * 7 + (P(), weights, weights),
        out_specs=(rows, rows, weights, weights),
        check_vma=False,
    )
```

time: 208 us -> 173 us (0.83)
  Pallas kernels: 190 us -> 156 us
    pallas_call x1, Pallas kernels: 190 us -> 156 us  [per_device(): pl.pallas_call(kernel, out_shape=(jax.ShapeDtypeStruct((tokens, width), b...]
where the time goes in v4:
time: 173 us; the launch traced here: 172 us
  Pallas kernels  156 us (90%)
  local copies, waits for them, and re-layouts  11.2 us (6%)
  other arithmetic  4.41 us (3%)
    pallas_call x1, Pallas kernels, per_device(): pl.pallas_call(kernel, out_shape=(jax.ShapeDtypeStruct((tokens, width), b...  156 us
    unnamed x6, local copies, waits for them, and re-layouts  9.92 us

profile of v4, /device:TPU:1, one launch (start us, length us, event | category | flops | bytes accessed | tf_op | source)
XLA Modules:
  0.0 172.4 jit_solution(3115352423779268572)
XLA Ops:
  0.7 0.8 compare_reduce_fusion.1
  1.5 0.8 compare_reduce_fusion
  2.3 1.3 reshape.217.gain
  3.6 0.2 fusion
  3.8 0.2 fusion.1
  4.0 0.8 fusion.3
  4.8 0.6 pad_maximum_fusion.1.tab_b
  5.4 0.8 fusion.2
  6.2 0.6 pad_maximum_fusion.tab_f
  6.8 155.6 %shard_map.129 = (bf16[128,1536]{1,0:T(8,128)(2,1)}, bf16[128,1536]{1,0:T(8,128)(2,1)}, bf16[1536,1536]{1,0:T(8,128)(2,1)}, bf16[768,1536]{1,0:T(8,128)(2,1)}) custom-call(bf16[128,1536]{1,0:T(8,128)(2,1)} %x_f.1, bf16[128,1536]{1,0:T(8,128)(2,1)} %x_b.1, bf16[128,1536]{1,0:T(8,128)(2,1)} %cot.1, f32[1,1536]{1,0:T(1,128)} %reshape.217.gain, ...), custom_call_target="tpu_custom_call" | custom-call | tf_op jit(solution)/shard_map/pallas_call | solution.py:443
  162.5 1.8 %copy.22 = bf16[128,1536]{1,0:T(8,128)(2,1)} copy(bf16[128,1536]{1,0:T(8,128)(2,1)} %get-tuple-element.18) | data formatting | bytes 786432
  164.2 1.8 %copy.23 = bf16[128,1536]{1,0:T(8,128)(2,1)} copy(bf16[128,1536]{1,0:T(8,128)(2,1)} %get-tuple-element.19) | data formatting | bytes 786432
  166.0 0.0 copy-start
  166.0 5.0 %copy.24 = bf16[1,1,1536,1536]{3,2,1,0:T(8,128)(2,1)} copy(bf16[1,1,1536,1536]{3,2,1,0:T(8,128)(2,1)} %bitcast.22) | data formatting | bytes 9437184
  171.0 0.0 copy-done
  171.0 1.4 copy.25
  (2 shorter events, 0.0 us)
Async XLA Ops:
  166.0 5.0 %copy-start = (bf16[768,1536]{1,0:T(8,128)(2,1)S(1)}, bf16[768,1536]{1,0:T(8,128)(2,1)}, u32[]{:S(2)}) copy-start(bf16[768,1536]{1,0:T(8,128)(2,1)} %get-tuple-element.11) | copy-start | bytes 7077892

commit v5 on v4

--- a/solution.py
+++ b/solution.py
@@ -45,7 +45,7 @@
 def kernel(
     x_f, x_b, cot, gain, tab_f, tab_b, w_gu, w_dn,
     y_out, dx_out, grad_gu, grad_dn,
-    zx, ztab, mx, mc, mtab, normed, pick_f, pick_b, sent_f, sent_h, sent_c, got_f, got_h, got_c,
+    zx, ztab, mx, mc, mtab, normed, pick_f, pick_b, pick_e, sent_f, sent_h, sent_c, got_f, got_h, got_c,
     gu, dn, out_f, out_dh, back_f, back_dh, hid_f, hid, dboth, lhs_t, gout, sums_f, sums_b, total,
     w_sem, own_sem, zs_sem, zr_sem, ms_sem, mr_sem, fs_sem, fr_sem, hs_sem, hr_sem, cs_sem, cr_sem,
     ds_sem, dr_sem, es_sem, er_sem, qs_sem, qr_sem, ps_sem, pr_sem, g_sem,
@@ -65,7 +65,7 @@
 
     barrier = pltpu.get_barrier_semaphore()
     others = [(kz, 0, kc, 0) for kc in range(2) for kz in range(4)][1:]
-    others += [(0, 1, 0, 0), (0, 1, 1, 0), (0, 0, 0, 1), (0, 1, 0, 1)]
+    others += [(0, n % 2, (n // 2) % 2, n // 4) for n in (1, 3, 4, 5, 6, 7)]
     for other in others:
         pl.semaphore_signal(barrier, inc=1, device_id=peer(*other), device_id_type=MESH)
 
@@ -108,11 +108,13 @@
 
     def over_x(r):
         to = peer(0, r % 2, 0, r // 2)
+        by = peer(0, 1, 0, 1) if r == 2 else to
         i = r - 1
+        rows, cots = (mx.at[0], mc.at[0]) if r == 2 else (x_b, cot)
         return [
-            remote(x_b, mx.at[i], ms_sem.at[0, i], mr_sem.at[0, i], to),
-            remote(cot, mc.at[i], ms_sem.at[1, i], mr_sem.at[1, i], to),
             remote(tab_b.at[r], mtab.at[i], ms_sem.at[2, i], mr_sem.at[2, i], to),
+            remote(rows, mx.at[i], ms_sem.at[0, i], mr_sem.at[0, i], by),
+            remote(cots, mc.at[i], ms_sem.at[1, i], mr_sem.at[1, i], by),
         ]
 
     raw_z = [over_z(k) for k in (1, 2, 3)]
@@ -143,16 +145,12 @@
         pltpu.make_async_copy(sent_h.at[first], got_h.at[first], own_sem.at[0, r]).start()
         pltpu.make_async_copy(sent_c.at[first], got_c.at[first], own_sem.at[1, r]).start()
 
-    def return_bwd(r):
-        def go(j, _):
-            to = peer(-(j % 4), 0, j // 4, 0)
-            rows = pl.ds(r * PIECE + j * CAP, CAP)
-            remote(out_dh.at[rows], back_dh.at[rows], es_sem.at[r], er_sem.at[r], to).start()
-            return 0
-
-        lax.fori_loop(1, 8, go, 0)
-        first = pl.ds(r * PIECE, CAP)
-        pltpu.make_async_copy(out_dh.at[first], back_dh.at[first], own_sem.at[2, r]).start()
+    def return_bwd(r, kc):
+        i = r * 2 + kc
+        return remote(
+            out_dh.at[i], back_dh.at[i], es_sem.at[i - 1], er_sem.at[i - 1],
+            peer(0, r % 2, kc, r // 2),
+        )
 
     def rest(r):
         return pl.ds(r * PIECE + CAP, PIECE - CAP)
@@ -198,7 +196,8 @@
 
         def second(t):
             cols = pl.ds(pl.multiple_of(t * TILE, TILE), TILE)
-            out_dh[rows, cols] = dot_nt(dboth[rows, :], gu[half, cols, :]).astype(bf16)
+            dh = dot_nt(dboth[rows, :], gu[half, cols, :]).astype(bf16)
+            out_dh[2 * r : 2 * r + 2, :, :, cols] = dh.reshape(2, 4, CAP, TILE)
 
         loop(width // TILE, second)
 
@@ -240,11 +239,10 @@
 
     normalize(x_b, normed)
     pl.semaphore_wait(barrier, len(others))
-    for copies in raw_z + [raw_x[0], raw_x[2], raw_x[1]]:
+    for copies in (raw_z[0], raw_z[2], raw_z[1], raw_x[0], raw_x[2], raw_x[1][:1]):
         for copy in copies:
             copy.start()
     dispatch_bwd(0, tab_b.at[0], cot)
-    send_bwd(0)
 
     normalize(x_f, normed)
     dispatch_fwd(0, tab_f.at[0])
@@ -258,28 +256,29 @@
     ]
     for copy in own_f:
         copy.start()
-    for slot in (2, 3, 1):
-        for e in range(2):
+    for e in range(2):
+        for slot in (2, 3, 1):
             send_fwd(e, slot).start()
-    for r in (1, 3, 2):
+    for r in (1, 3):
         for copy in raw_x[r - 1]:
             copy.wait_recv()
+        if r == 1:
+            for copy in raw_x[1][1:]:
+                copy.start()
         normalize(mx.at[r - 1], normed)
         dispatch_bwd(r, mtab.at[r - 1], mc.at[r - 1])
         send_bwd(r)
     for copy in weights + own_f:
         copy.wait()
 
-    def forward(a):
-        for e in range(2):
-            for slot in (2 * a, 2 * a + 1):
-                if slot:
-                    send_fwd(e, slot).wait_recv()
-        for e in range(2):
-            forward_piece(a, e)
-            for slot in (2 * a, 2 * a + 1):
-                if slot:
-                    return_fwd(e, slot).start()
+    def forward(a, e):
+        for slot in (2 * a, 2 * a + 1):
+            if slot:
+                send_fwd(e, slot).wait_recv()
+        forward_piece(a, e)
+        for slot in (2 * a, 2 * a + 1):
+            if slot:
+                return_fwd(e, slot).start()
 
     def backward(r):
         landed(got_h.at[rest(r)], hs_sem.at[r], hr_sem.at[r]).wait_recv()
@@ -287,61 +286,50 @@
         pltpu.make_async_copy(all_of(sent_h, r), all_of(got_h, r), own_sem.at[0, r]).wait()
         pltpu.make_async_copy(all_of(sent_c, r), all_of(got_c, r), own_sem.at[1, r]).wait()
         backward_chain(r)
-        return_bwd(r)
-
-    forward(0)
+        for kc in range(2):
+            if r or kc:
+                return_bwd(r, kc).start()
+
+    forward(0, 0)
+    for copy in raw_x[1]:
+        copy.wait_recv()
+    normalize(mx.at[1], normed)
+    dispatch_bwd(2, mtab.at[1], mc.at[1])
+    send_bwd(2)
+    send_bwd(0)
+    forward(0, 1)
+    forward(1, 0)
+    backward(1)
+    forward(1, 1)
+    backward(3)
+    backward(2)
+    for b in range(4):
+        picks((tab_f.at[0] if b == 0 else ztab.at[b - 1])[2], pick_e.at[b])
     backward(0)
-    backward(1)
-    forward(1)
     home = [
         pltpu.make_async_copy(out_f.at[e, 0], back_f.at[e * 4], own_sem.at[3, e]) for e in range(2)
     ]
+    home.append(pltpu.make_async_copy(out_dh.at[0], back_dh.at[0], own_sem.at[2, 0]))
     for copy in home:
         copy.start()
-    backward(3)
-    backward(2)
-    strips(hid, got_c, units // TILE, grad_dn, 1)
-
-    def returned(r):
-        return landed(back_dh.at[rest(r)], es_sem.at[r], er_sem.at[r])
-
-    def gathered_bwd(r, cols):
-        return dot(pick_b[r].T, back_dh[pl.ds(r * PIECE, PIECE), cols])
-
-    def home_bwd(r):
-        returned(r).wait_recv()
-        pltpu.make_async_copy(all_of(out_dh, r), all_of(back_dh, r), own_sem.at[2, r]).wait()
-
-    back_x = []
-    for r in (1, 3, 2):
-        home_bwd(r)
-
-        def sum_block(cols):
-            mx[r - 1, :, cols] = gathered_bwd(r, cols).astype(bf16)
-
-        wide(sum_block)
-        copy = remote(
-            mx.at[r - 1], sums_b.at[r - 1], ps_sem.at[r - 1], pr_sem.at[r - 1],
-            peer(0, r % 2, 0, r // 2),
-        )
-        copy.start()
-        back_x.append(copy)
+
+    def gated_rows(b, table):
+        gates = slot_gates(table[1], pick_f.at[b])
+        rows = back_f[:, b].reshape(PIECE, width).astype(f32) * gates
+        lhs = rows.astype(bf16)
+        back_f[:, b] = lhs.reshape(8, CAP, width)
+
+    def gathered_fwd(b, cols):
+        return dot(pick_f[b].T, back_f[:, b, :, cols].reshape(PIECE, WIDE))
+
+    def gathered_bwd(b, cols):
+        return dot(pick_e[b].T, back_dh[:, b, :, cols].reshape(PIECE, WIDE))
 
     for e in range(2):
         for slot in (1, 2, 3):
             return_fwd(e, slot).wait_recv()
     for copy in home:
         copy.wait()
-
-    def gated_rows(b, table):
-        gates = slot_gates(table[1], pick_f.at[b])
-        rows = back_f[:, b].reshape(PIECE, width).astype(f32) * gates
-        lhs = rows.astype(bf16)
-        back_f[:, b] = lhs.reshape(8, CAP, width)
-
-    def gathered_fwd(b, cols):
-        return dot(pick_f[b].T, back_f[:, b, :, cols].reshape(PIECE, WIDE))
-
     back_z = []
     for b in (2, 1, 3):
         gated_rows(b, ztab.at[b - 1])
@@ -355,16 +343,32 @@
         )
         copy.start()
         back_z.append(copy)
-    gated_rows(0, tab_f.at[0])
-
-    strips(got_h, dboth, width // TILE, grad_gu, 0)
-
-    home_bwd(0)
+
+    for copy in raw_x[1][1:]:
+        copy.wait_send()
+    for i in range(1, 8):
+        return_bwd(i // 2, i % 2).wait_recv()
+    back_x = []
+    for b in (2, 1, 3):
+
+        def sum_block(cols):
+            mx[b - 1, :, cols] = gathered_bwd(b, cols).astype(bf16)
+
+        wide(sum_block)
+        copy = remote(
+            mx.at[b - 1], sums_b.at[b - 1], ps_sem.at[b - 1], pr_sem.at[b - 1], peer(-b, 0, 0, 0)
+        )
+        copy.start()
+        back_x.append(copy)
 
     def own_dh(cols):
         total[:, cols] = gathered_bwd(0, cols)
 
     wide(own_dh)
+    gated_rows(0, tab_f.at[0])
+    strips(hid, got_c, units // TILE, grad_dn, 1)
+    strips(got_h, dboth, width // TILE, grad_gu, 0)
+
     for copy in back_z:
         copy.wait_recv()
 
@@ -392,7 +396,7 @@
 
     loop(x_b.shape[0] // 32, finish)
 
-    for copies in raw_z + raw_x:
+    for copies in raw_z + [raw_x[0], raw_x[2], raw_x[1][:1]]:
         for copy in copies:
             copy.wait_send()
     for copy in back_x + back_z:
@@ -404,7 +408,8 @@
     for r in range(4):
         landed(got_h.at[rest(r)], hs_sem.at[r], hr_sem.at[r]).wait_send()
         landed(got_c.at[rest(r)], cs_sem.at[r], cr_sem.at[r]).wait_send()
-        returned(r).wait_send()
+    for i in range(1, 8):
+        return_bwd(i // 2, i % 2).wait_send()
 
 
 def slot_table(routes, gates, experts):
@@ -431,6 +436,9 @@
     d_b = ((z + s % 4) % 4) * 4 + ((xl + agent % 2) % 2) * 2 + core
     table_f = slot_table(route_fwd, gate_fwd, 2 * d_f + s // 4)
     table_b = slot_table(route_bwd, gate_bwd, 2 * d_b + (half + agent // 2) % 2)
+
+    by_z = table_b[:, 0].reshape(4, 2, 4, tokens).transpose(2, 0, 1, 3).reshape(4, 1, 8, tokens)
+    table_f = jnp.concatenate([table_f, by_z], axis=1)
 
     rows = 32 * CAP
     anywhere = pl.BlockSpec(memory_space=pl.ANY)
@@ -452,11 +460,12 @@
         out_specs=(vmem, vmem, anywhere, anywhere),
         scratch_shapes=[
             hold(3, tokens, width),
-            hold(3, 2, 8, tokens, dtype=f32),
+            hold(3, 3, 8, tokens, dtype=f32),
             hold(3, tokens, width),
             hold(3, tokens, width),
             hold(3, 2, 8, tokens, dtype=f32),
             hold(tokens, width),
+            hold(4, PIECE, tokens),
             hold(4, PIECE, tokens),
             hold(4, PIECE, tokens),
             hold(8, 4, CAP, width),
@@ -468,9 +477,9 @@
             hold(2, width, width),
             hold(2, units, width),
             hold(2, 4, 4, CAP, width),
-            hold(rows, width),
             hold(8, 4, CAP, width),
-            hold(rows, width),
+            hold(8, 4, CAP, width),
+            hold(8, 4, CAP, width),
             hold(PIECE, units),
             hold(rows, units),
             hold(rows, width),
@@ -481,7 +490,7 @@
             hold(tokens, width, dtype=f32),
             dma((2,)), dma((4, 4)), dma((2, 3)), dma((2, 3)), dma((3, 3)), dma((3, 3)),
             dma((2, 3)), dma((2, 3)), dma((4,)), dma((4,)), dma((4,)), dma((4,)),
-            dma((2, 3)), dma((2, 3)), dma((4,)), dma((4,)), dma((3,)), dma((3,)),
+            dma((2, 3)), dma((2, 3)), dma((7,)), dma((7,)), dma((3,)), dma((3,)),
             dma((3,)), dma((3,)), dma((2,)),
         ],
         compiler_params=pltpu.CompilerParams(

time: 173 us -> 185 us (1.069)
  Pallas kernels: 156 us -> 168 us
    pallas_call x1, Pallas kernels: 156 us -> 168 us  [per_device(): pl.pallas_call(kernel, out_shape=(jax.ShapeDtypeStruct((tokens, width), b...]
where the time goes in v5:
time: 185 us; the launch traced here: 184 us
  Pallas kernels  168 us (91%)
  local copies, waits for them, and re-layouts  11.2 us (6%)
  other arithmetic  4.42 us (2%)
    pallas_call x1, Pallas kernels, per_device(): pl.pallas_call(kernel, out_shape=(jax.ShapeDtypeStruct((tokens, width), b...  168 us
    unnamed x6, local copies, waits for them, and re-layouts  9.92 us

profile of v5, /device:TPU:1, one launch (start us, length us, event | category | flops | bytes accessed | tf_op | source)
XLA Modules:
  0.0 184.3 jit_solution(17016456715551744971)
XLA Ops:
  0.7 0.8 compare_reduce_fusion.1
  1.5 0.8 compare_reduce_fusion
  2.3 1.3 reshape.220.gain
  3.6 0.2 convolution_select_fusion
  3.8 0.2 fusion
  4.0 0.8 fusion.2
  4.8 0.8 fusion.1
  5.6 0.6 pad_maximum_fusion.1.tab_b
  6.2 0.6 pad_maximum_fusion.tab_f
  6.9 167.5 %shard_map.129 = (bf16[128,1536]{1,0:T(8,128)(2,1)}, bf16[128,1536]{1,0:T(8,128)(2,1)}, bf16[1536,1536]{1,0:T(8,128)(2,1)}, bf16[768,1536]{1,0:T(8,128)(2,1)}) custom-call(bf16[128,1536]{1,0:T(8,128)(2,1)} %x_f.1, bf16[128,1536]{1,0:T(8,128)(2,1)} %x_b.1, bf16[128,1536]{1,0:T(8,128)(2,1)} %cot.1, f32[1,1536]{1,0:T(1,128)} %reshape.220.gain, ...), custom_call_target="tpu_custom_call" | custom-call | tf_op jit(solution)/shard_map/pallas_call | solution.py:451
  174.4 1.8 copy.24
  176.2 1.8 copy.25
  177.9 0.0 copy-start
  177.9 5.0 %copy.26 = bf16[1,1,1536,1536]{3,2,1,0:T(8,128)(2,1)} copy(bf16[1,1,1536,1536]{3,2,1,0:T(8,128)(2,1)} %bitcast.24) | data formatting | bytes 9437184
  182.9 0.0 copy-done
  182.9 1.4 copy.27
  (3 shorter events, 0.0 us)
Async XLA Ops:
  177.9 5.0 %copy-start = (bf16[768,1536]{1,0:T(8,128)(2,1)S(1)}, bf16[768,1536]{1,0:T(8,128)(2,1)}, u32[]{:S(2)}) copy-start(bf16[768,1536]{1,0:T(8,128)(2,1)} %get-tuple-element.11) | copy-start | bytes 7077892

commit v6 on v4

--- a/solution.py
+++ b/solution.py
@@ -43,11 +43,11 @@
 
 
 def kernel(
-    x_f, x_b, cot, gain, tab_f, tab_b, w_gu, w_dn,
+    x_f, x_b, cot, gain, routes_f, gates_f, routes_b, gates_b, w_gu, w_dn,
     y_out, dx_out, grad_gu, grad_dn,
-    zx, ztab, mx, mc, mtab, normed, pick_f, pick_b, sent_f, sent_h, sent_c, got_f, got_h, got_c,
+    tab_f, tab_b, zx, ztab, mx, mc, mtab, normed, pick_f, pick_b, sent_f, sent_h, sent_c, got_f, got_h, got_c,
     gu, dn, out_f, out_dh, back_f, back_dh, hid_f, hid, dboth, lhs_t, gout, sums_f, sums_b, total,
-    w_sem, own_sem, zs_sem, zr_sem, ms_sem, mr_sem, fs_sem, fr_sem, hs_sem, hr_sem, cs_sem, cr_sem,
+    w_sem, own_sem, rs_sem, rr_sem, zs_sem, zr_sem, ms_sem, mr_sem, fs_sem, fr_sem, hs_sem, hr_sem, cs_sem, cr_sem,
     ds_sem, dr_sem, es_sem, er_sem, qs_sem, qr_sem, ps_sem, pr_sem, g_sem,
 ):
     width = got_h.shape[1]
@@ -81,9 +81,23 @@
             rows = pl.ds(pl.multiple_of(i * 32, 32), 32)
             v = src[rows, :].astype(f32)
             scale = lax.rsqrt(jnp.mean(v * v, axis=-1, keepdims=True) + norm_eps)
-            dst[rows, :] = (v * scale * gain[...]).astype(bf16)
+            dst[rows, :] = (v * scale * gain[...][None, :]).astype(bf16)
 
         loop(src.shape[0] // 32, some)
+
+    def tables(routes, gates, experts, dst):
+        chosen = jnp.zeros((32, 128), f32)
+        weight = jnp.zeros((32, 128), f32)
+        for n in range(routes.shape[0]):
+            hit = routes[n : n + 1, :] == experts
+            chosen = jnp.where(hit, 1.0, chosen)
+            weight = jnp.where(hit, gates[n : n + 1, :], weight)
+        row = lax.broadcasted_iota(jnp.int32, (128, 128), 0)
+        col = lax.broadcasted_iota(jnp.int32, (128, 128), 1)
+        earlier = jnp.where(row < col, 1.0, 0.0).astype(bf16)
+        slots = jnp.where(chosen > 0.0, dot(chosen.astype(bf16), earlier), -1.0)
+        dst[:, 0] = slots.reshape(4, 8, 128)
+        dst[:, 1] = weight.reshape(4, 8, 128)
 
     def picks(slots, dst):
         want = lax.broadcasted_iota(jnp.int32, (8, CAP, 128), 1).astype(f32)
@@ -98,13 +112,22 @@
         loop(width // WIDE, lambda t: body(pl.ds(pl.multiple_of(t * WIDE, WIDE), WIDE)))
 
     def over_z(k):
-        return [
-            remote(x_f, zx.at[k - 1], zs_sem.at[0, k - 1], zr_sem.at[0, k - 1], peer(k, 0, 0, 0)),
-            remote(
-                tab_f.at[k], ztab.at[k - 1], zs_sem.at[1, k - 1], zr_sem.at[1, k - 1],
-                peer(k, 0, 0, 0),
-            ),
-        ]
+        table = remote(
+            tab_f.at[k], ztab.at[k - 1], zs_sem.at[1, k - 1], zr_sem.at[1, k - 1], peer(k, 0, 0, 0)
+        )
+        if k == 2:
+            return [table]
+        rows = remote(
+            x_f, zx.at[k - 1], zs_sem.at[0, k - 1], zr_sem.at[0, k - 1], peer(k, 0, 0, 0)
+        )
+        return [table, rows]
+
+    def relay(k):
+        part = pl.ds(0 if k == 1 else 64, 64)
+        i = k // 2
+        return remote(
+            zx.at[k - 1, part], zx.at[1, part], rs_sem.at[i], rr_sem.at[i], peer(k, 0, 0, 0)
+        )
 
     def over_x(r):
         to = peer(0, r % 2, 0, r // 2)
@@ -117,6 +140,7 @@
 
     raw_z = [over_z(k) for k in (1, 2, 3)]
     raw_x = [over_x(r) for r in (1, 2, 3)]
+    relays = [relay(1), relay(3)]
 
     def send_fwd(e, slot):
         return remote(
@@ -238,19 +262,31 @@
 
         wide(some)
 
+    _, _, z, xl, c = place()
+    k = lax.broadcasted_iota(jnp.int32, (32, 128), 0)
+    agent, s = k >> 3, k & 7
+    d_f = ((z + agent) & 3) * 4 + ((xl + (s >> 1)) & 1) * 2 + ((c + s) & 1)
+    d_b = ((z + s) & 3) * 4 + ((xl + agent) & 1) * 2 + ((c + (s >> 2)) & 1)
+    tables(routes_f, gates_f, 2 * d_f + (s >> 2), tab_f)
+    tables(routes_b, gates_b, 2 * d_b + ((half + (agent >> 1)) & 1), tab_b)
     normalize(x_b, normed)
     pl.semaphore_wait(barrier, len(others))
     for copies in raw_z + [raw_x[0], raw_x[2], raw_x[1]]:
         for copy in copies:
             copy.start()
     dispatch_bwd(0, tab_b.at[0], cot)
-    send_bwd(0)
 
     normalize(x_f, normed)
     dispatch_fwd(0, tab_f.at[0])
+    for k, copy in zip((1, 3), relays):
+        for raw in raw_z[k - 1]:
+            raw.wait_recv()
+        copy.start()
+    send_bwd(0)
     for k in (1, 3, 2):
-        for copy in raw_z[k - 1]:
-            copy.wait_recv()
+        if k == 2:
+            for copy in raw_z[1] + relays:
+                copy.wait_recv()
         normalize(zx.at[k - 1], normed)
         dispatch_fwd(k, ztab.at[k - 1])
     own_f = [
@@ -342,6 +378,8 @@
     def gathered_fwd(b, cols):
         return dot(pick_f[b].T, back_f[:, b, :, cols].reshape(PIECE, WIDE))
 
+    for copy in relays:
+        copy.wait_send()
     back_z = []
     for b in (2, 1, 3):
         gated_rows(b, ztab.at[b - 1])
@@ -386,7 +424,7 @@
         dh = total[rows, :]
         for n in range(3):
             dh = dh + sums_b[n, rows, :].astype(f32)
-        q = gain[...] * dh
+        q = gain[...][None, :] * dh
         dx = scale * (q - hat * jnp.mean(hat * q, axis=-1, keepdims=True))
         dx_out[rows, :] = dx.astype(bf16)
 
@@ -407,14 +445,24 @@
         returned(r).wait_send()
 
 
-def slot_table(routes, gates, experts):
-    names = routes[:, :, None] == experts[None, None, :]
-    chosen = jnp.any(names, axis=1)
-    gate = jnp.sum(jnp.where(names, gates[:, :, None], 0.0), axis=1)
-    tokens = routes.shape[0]
-    earlier = jnp.tri(tokens, tokens, -1, dtype=bf16)
-    slot = jnp.where(chosen, dot(earlier, chosen.astype(bf16)), -1.0)
-    return jnp.stack([slot.T.reshape(4, 8, tokens), gate.T.reshape(4, 8, tokens)], axis=1)
+def writer(*refs):
+    sems = refs[-1]
+    held = refs[8:-1]
+    reads, writes = [], []
+    for n in range(4):
+        src, dst, buf = refs[n], refs[4 + n], held[n]
+        for at in range(0, src.shape[0], TILE):
+            rows = pl.ds(at, min(TILE, src.shape[0] - at))
+            i = len(reads)
+            reads.append(pltpu.make_async_copy(src.at[rows], buf.at[rows], sems.at[0, i]))
+            writes.append(pltpu.make_async_copy(buf.at[rows], dst.at[rows], sems.at[1, i]))
+    for copy in reads:
+        copy.start()
+    for read, write in zip(reads, writes):
+        read.wait()
+        write.start()
+    for copy in writes:
+        copy.wait()
 
 
 def per_device(
@@ -423,15 +471,6 @@
     tokens, width = x_fwd.shape
     units = w_down.shape[2]
 
-    _, half, z, xl, c = place()
-    k = jnp.arange(32, dtype=jnp.int32)
-    agent, s = k // 8, k % 8
-    core = (c + s // 4) % 2
-    d_f = ((z + agent) % 4) * 4 + ((xl + (s // 2) % 2) % 2) * 2 + (c + s % 2) % 2
-    d_b = ((z + s % 4) % 4) * 4 + ((xl + agent % 2) % 2) * 2 + core
-    table_f = slot_table(route_fwd, gate_fwd, 2 * d_f + s // 4)
-    table_b = slot_table(route_bwd, gate_bwd, 2 * d_b + (half + agent // 2) % 2)
-
     rows = 32 * CAP
     anywhere = pl.BlockSpec(memory_space=pl.ANY)
     vmem = pl.BlockSpec(memory_space=pltpu.VMEM)
@@ -440,7 +479,7 @@
     def hold(*shape, dtype=bf16):
         return pltpu.VMEM(shape, dtype)
 
-    y_fwd, dx_bwd, grad_gu, grad_dn = pl.pallas_call(
+    results = pl.pallas_call(
         kernel,
         out_shape=(
             jax.ShapeDtypeStruct((tokens, width), bf16),
@@ -448,9 +487,11 @@
             jax.ShapeDtypeStruct((width, width), bf16),
             jax.ShapeDtypeStruct((units, width), bf16),
         ),
-        in_specs=[vmem] * 6 + [anywhere] * 2,
+        in_specs=[vmem] * 8 + [anywhere] * 2,
         out_specs=(vmem, vmem, anywhere, anywhere),
         scratch_shapes=[
+            hold(4, 2, 8, tokens, dtype=f32),
+            hold(4, 2, 8, tokens, dtype=f32),
             hold(3, tokens, width),
             hold(3, 2, 8, tokens, dtype=f32),
             hold(3, tokens, width),
@@ -479,7 +520,7 @@
             hold(3, tokens, width),
             hold(3, tokens, width),
             hold(tokens, width, dtype=f32),
-            dma((2,)), dma((4, 4)), dma((2, 3)), dma((2, 3)), dma((3, 3)), dma((3, 3)),
+            dma((2,)), dma((4, 4)), dma((2,)), dma((2,)), dma((2, 3)), dma((2, 3)), dma((3, 3)), dma((3, 3)),
             dma((2, 3)), dma((2, 3)), dma((4,)), dma((4,)), dma((4,)), dma((4,)),
             dma((2, 3)), dma((2, 3)), dma((4,)), dma((4,)), dma((3,)), dma((3,)),
             dma((3,)), dma((3,)), dma((2,)),
@@ -491,12 +532,22 @@
         x_fwd,
         x_bwd,
         cotangent,
-        norm_gain.reshape(1, width),
-        table_f,
-        table_b,
+        norm_gain,
+        route_fwd.T,
+        gate_fwd.T,
+        route_bwd.T,
+        gate_bwd.T,
         w_gate_up[0],
         w_down[0],
     )
+    y_fwd, dx_bwd, grad_gu, grad_dn = pl.pallas_call(
+        writer,
+        out_shape=tuple(jax.ShapeDtypeStruct(r.shape, r.dtype) for r in results),
+        in_specs=[anywhere] * 4,
+        out_specs=(anywhere,) * 4,
+        scratch_shapes=[hold(*r.shape) for r in results] + [dma((2, 11))],
+        compiler_params=pltpu.CompilerParams(vmem_limit_bytes=67043328),
+    )(*results)
     return y_fwd, dx_bwd, grad_gu[None, None], grad_dn[None, None]
 
 

time: 173 us -> 158 us (0.913)
  local copies, waits for them, and re-layouts: 11.2 us -> 0 us
  other arithmetic: 4.41 us -> 0 us
    unnamed x6 -> x0, local copies, waits for them, and re-layouts: 9.92 us -> none
    pallas_call x0 -> x1, Pallas kernels: none -> 6.11 us  [per_device(): pl.pallas_call(writer, out_shape=tuple((jax.ShapeDtypeStruct(r.shape, r.d...]
    pallas_call x1, Pallas kernels: 156 us -> 151 us  [per_device(): pl.pallas_call(kernel, out_shape=(jax.ShapeDtypeStruct((tokens, width), b...]
where the time goes in v6:
time: 158 us
  Pallas kernels  157 us (99%)
    pallas_call x1, Pallas kernels, per_device(): pl.pallas_call(kernel, out_shape=(jax.ShapeDtypeStruct((tokens, width), b...  151 us
    pallas_call x1, Pallas kernels, per_device(): pl.pallas_call(writer, out_shape=tuple((jax.ShapeDtypeStruct(r.shape, r.d...  6.11 us

profile of v6, /device:TPU:1, one launch (start us, length us, event | category | flops | bytes accessed | tf_op | source)
XLA Modules:
  0.0 158.0 jit_solution(4776961609218856030)
XLA Ops:
  0.6 151.3 %shard_map.129 = (bf16[128,1536]{1,0:T(8,128)(2,1)}, bf16[128,1536]{1,0:T(8,128)(2,1)}, bf16[1536,1536]{1,0:T(8,128)(2,1)}, bf16[768,1536]{1,0:T(8,128)(2,1)}) custom-call(bf16[128,1536]{1,0:T(8,128)(2,1)} %x_f.1, bf16[128,1536]{1,0:T(8,128)(2,1)} %x_b.1, bf16[128,1536]{1,0:T(8,128)(2,1)} %cot.1, f32[1536]{0:T(1024)} %gain.1, s32[6,128]{1,0:T(8,128)} %bitcast.10, ...), custom_call_target="tpu_custom_call" | custom-call | tf_op jit(solution)/shard_map/pallas_call | solution.py:482
  151.9 6.1 %shard_map.130 = (bf16[128,1536]{1,0:T(8,128)(2,1)}, bf16[128,1536]{1,0:T(8,128)(2,1)}, bf16[1536,1536]{1,0:T(8,128)(2,1)}, bf16[768,1536]{1,0:T(8,128)(2,1)}) custom-call(bf16[128,1536]{1,0:T(8,128)(2,1)} %get-tuple-element.12.refs_0_, bf16[128,1536]{1,0:T(8,128)(2,1)} %get-tuple-element.13.refs_1_, bf16[1536,1536]{1,0:T(8,128)(2,1)} %get-tuple-element.14.refs_2_, ...), custom_call_target="tpu_custom_call" | custom-call | tf_op jit(solution)/shard_map/pallas_call | solution.py:543

commit v7 on v6

--- a/solution.py
+++ b/solution.py
@@ -226,21 +226,24 @@
 
         loop(width // TILE, second)
 
-    def strips(lhs, rhs, count, dst, buf):
-        def strip(m):
-            at = pl.multiple_of(m * TILE, TILE)
-            lhs_t[...] = lhs[:, pl.ds(at, TILE)].T
+    def strips(lhs, rhs, which, dst):
+        copies = []
+        for n, m in enumerate(which):
+            rows = pl.ds(m * TILE, TILE)
+            buf = n % 2
+            lhs_t[...] = lhs[:, rows].T
+            if n >= 2:
+                copies[n - 2].wait()
 
             def cols_of(t):
                 cols = pl.ds(pl.multiple_of(t * TILE, TILE), TILE)
                 gout[buf, :, cols] = dot(lhs_t[...], rhs[:, cols]).astype(bf16)
 
             loop(width // TILE, cols_of)
-            copy = pltpu.make_async_copy(gout.at[buf], dst.at[pl.ds(at, TILE)], g_sem.at[buf])
-            copy.start()
+            copies.append(pltpu.make_async_copy(gout.at[buf], dst.at[rows], g_sem.at[buf]))
+            copies[n].start()
+        for copy in copies[-2:]:
             copy.wait()
-
-        loop(count, strip)
 
     def dispatch_fwd(b, table):
         picks(table[0], pick_f.at[b])
@@ -326,7 +329,6 @@
         return_bwd(r)
 
     forward(0)
-    backward(0)
     backward(1)
     forward(1)
     home = [
@@ -336,7 +338,8 @@
         copy.start()
     backward(3)
     backward(2)
-    strips(hid, got_c, units // TILE, grad_dn, 1)
+    backward(0)
+    strips(hid, got_c, range(units // TILE), grad_dn)
 
     def returned(r):
         return landed(back_dh.at[rest(r)], es_sem.at[r], er_sem.at[r])
@@ -395,7 +398,7 @@
         back_z.append(copy)
     gated_rows(0, tab_f.at[0])
 
-    strips(got_h, dboth, width // TILE, grad_gu, 0)
+    strips(got_h, dboth, range(width // TILE), grad_gu)
 
     home_bwd(0)
 

time: 158 us -> 154 us (0.975)
  Pallas kernels: 157 us -> 153 us
    pallas_call x1, Pallas kernels: 151 us -> 147 us  [per_device(): pl.pallas_call(kernel, out_shape=(jax.ShapeDtypeStruct((tokens, width), b...]
where the time goes in v7:
time: 154 us
  Pallas kernels  153 us (99%)
    pallas_call x1, Pallas kernels, per_device(): pl.pallas_call(kernel, out_shape=(jax.ShapeDtypeStruct((tokens, width), b...  147 us
    pallas_call x1, Pallas kernels, per_device(): pl.pallas_call(writer, out_shape=tuple((jax.ShapeDtypeStruct(r.shape, r.d...  6.11 us

profile of v7, /device:TPU:1, one launch (start us, length us, event | category | flops | bytes accessed | tf_op | source)
XLA Modules:
  0.0 153.5 jit_solution(11311404706815431996)
XLA Ops:
  0.6 146.8 %shard_map.129 = (bf16[128,1536]{1,0:T(8,128)(2,1)}, bf16[128,1536]{1,0:T(8,128)(2,1)}, bf16[1536,1536]{1,0:T(8,128)(2,1)}, bf16[768,1536]{1,0:T(8,128)(2,1)}) custom-call(bf16[128,1536]{1,0:T(8,128)(2,1)} %x_f.1, bf16[128,1536]{1,0:T(8,128)(2,1)} %x_b.1, bf16[128,1536]{1,0:T(8,128)(2,1)} %cot.1, f32[1536]{0:T(1024)} %gain.1, s32[6,128]{1,0:T(8,128)} %bitcast.10, ...), custom_call_target="tpu_custom_call" | custom-call | tf_op jit(solution)/shard_map/pallas_call | solution.py:485
  147.4 6.1 %shard_map.130 = (bf16[128,1536]{1,0:T(8,128)(2,1)}, bf16[128,1536]{1,0:T(8,128)(2,1)}, bf16[1536,1536]{1,0:T(8,128)(2,1)}, bf16[768,1536]{1,0:T(8,128)(2,1)}) custom-call(bf16[128,1536]{1,0:T(8,128)(2,1)} %get-tuple-element.12.refs_0_, bf16[128,1536]{1,0:T(8,128)(2,1)} %get-tuple-element.13.refs_1_, bf16[1536,1536]{1,0:T(8,128)(2,1)} %get-tuple-element.14.refs_2_, ...), custom_call_target="tpu_custom_call" | custom-call | tf_op jit(solution)/shard_map/pallas_call | solution.py:546
